TPU v7x, 32 devices: a whole 2x2x4 slice. The times are simulated.
32 devices in a mesh: group: 2 (over y), tile: 8 (over z, x), strip: 2 (over core).
Axes of the slice: x: 2, y: 2, z: 4, core: 2. Of those that a mesh axis runs over, the one named last changes fastest.
Arguments:
- image: bfloat16 [128, 256, 256], P(('group', 'strip'), 'tile'), parts along dimension 0, may hold values from -16 to 16
- bn_gain: float32 [256], replicated, may hold values from 0.25 to 1.75
- bn_shift: float32 [256], replicated, may hold values from -3 to 3
- w_expand: bfloat16 [256, 1024], replicated, may hold values from -0.375 to 0.375
- b_expand: float32 [1024], replicated, may hold values from -3 to 3
- w_depth: float32 [9, 1024], replicated, may hold values from -2 to 2
- b_depth: float32 [1024], replicated, may hold values from -3 to 3
- w_project: bfloat16 [1024, 256], replicated, may hold values from -0.1875 to 0.1875
- b_project: float32 [256], replicated, may hold values from -3 to 3
- attn_gain: float32 [256], replicated, may hold values from 0.25 to 1.75
- attn_shift: float32 [256], replicated, may hold values from -2 to 2
- w_qkv: bfloat16 [256, 768], replicated, may hold values from -0.375 to 0.375
- w_out: bfloat16 [256, 256], replicated, may hold values from -0.375 to 0.375
- rel_table: float32 [8, 225], replicated, may hold values from -4 to 304
- ffn_gain: float32 [256], replicated, may hold values from 0.25 to 1.75
- ffn_shift: float32 [256], replicated, may hold values from -2 to 2
- w_up: bfloat16 [256, 1024], replicated, may hold values from -0.375 to 0.375
- b_up: float32 [1024], replicated, may hold values from -3 to 3
- w_down: bfloat16 [1024, 256], replicated, may hold values from -0.1875 to 0.1875
- b_down: float32 [256], replicated, may hold values from -3 to 3
Outputs:
- block_out: bfloat16 [128, 256, 256], P(('group', 'strip'), 'tile'), parts along dimension 0
There are 2 independent parts, one for each index of `group`. A program takes and returns all parts, laid end to end along the dimension named above; an argument that names none is the same for every part. Nothing has to cross between parts.
All inputs are finite; a program needn't handle non-finite values.
Results may differ from a plain program's by a relative error of at most 0.0064.
Values may be sent and summed in bfloat16 or wider, within the bound.
A program may use at most 64 MiB of HBM per device.

v0:
```python
import jax
import jax.numpy as jnp
from jax import lax
from jax.sharding import PartitionSpec as P

GRID = 8


EPSILON = 1e-05


def padded(value, sides, width):
    for axis, dim in sides:
        devices, length = (lax.axis_size(axis), value.shape[dim])
        up = [(i, (i + 1) % devices) for i in range(devices - 1)]
        down = [(j, i) for i, j in up]
        last = lax.slice_in_dim(value, length - width, length, axis=dim)
        initial = lax.slice_in_dim(value, 0, width, axis=dim)
        before = lax.ppermute(last, axis, up)
        after = lax.ppermute(initial, axis, down)
        value = jnp.concatenate([before, value, after], axis=dim)
    return value


def gelu_tanh(inputs):
    return jax.nn.gelu(inputs, approximate=True)


def layer_norm(inputs, norm_gain, norm_shift):
    center = jnp.mean(inputs, axis=-1, keepdims=True)
    spread = jnp.mean(jnp.square(inputs - center), axis=-1, keepdims=True)
    return (inputs - center) * lax.rsqrt(spread + EPSILON) * norm_gain + norm_shift


def expand_tokens(pixels, bn_gain, bn_shift, w_expand, b_expand):
    normed = (pixels.astype(jnp.float32) * bn_gain + bn_shift).astype(jnp.bfloat16)
    pre_act = jnp.dot(normed, w_expand, preferred_element_type=jnp.float32) + b_expand
    return gelu_tanh(pre_act).astype(jnp.bfloat16)


def depthwise(framed, w_depth, b_depth):
    out_rows = framed.shape[0] - 2
    out_cols = framed.shape[1] - 2
    accum_sum = jnp.zeros((out_rows, out_cols, framed.shape[2]), jnp.float32) + b_depth
    for row_step in range(3):
        for col_step in range(3):
            window_part = framed[row_step : row_step + out_rows, col_step : col_step + out_cols]
            accum_sum = (
                accum_sum + window_part.astype(jnp.float32) * w_depth[row_step * 3 + col_step]
            )
    return gelu_tanh(accum_sum).astype(jnp.bfloat16)


def position_bias(rel_table):
    grid_side = GRID
    token_ids = jnp.arange(grid_side * grid_side, dtype=jnp.int32)
    row_of = token_ids // grid_side
    col_of = token_ids % grid_side
    offset = (row_of[:, None] - row_of[None, :] + grid_side - 1) * (2 * grid_side - 1) + (
        col_of[:, None] - col_of[None, :] + grid_side - 1
    )
    entry_ids = jnp.arange((2 * grid_side - 1) ** 2, dtype=jnp.int32)
    onehot = (offset.reshape(-1)[:, None] == entry_ids[None, :]).astype(jnp.float32)
    pos_bias = jnp.dot(
        rel_table, onehot.T, precision=lax.Precision.HIGHEST, preferred_element_type=jnp.float32
    )
    return pos_bias.reshape(rel_table.shape[0], grid_side * grid_side, grid_side * grid_side)


def grid_attention(windows, attn_gain, attn_shift, w_qkv, w_out, pos_bias):
    win_count = windows.shape[0]
    places = windows.shape[1]
    model_width = windows.shape[2]
    head_count = pos_bias.shape[0]
    head_size = model_width // head_count
    normed = layer_norm(windows.astype(jnp.float32), attn_gain, attn_shift).astype(jnp.bfloat16)
    projected_qkv = jnp.dot(normed, w_qkv, preferred_element_type=jnp.float32)
    queries = (projected_qkv[..., :model_width] * head_size ** (-0.5)).astype(jnp.bfloat16)
    key_heads = projected_qkv[..., model_width : 2 * model_width].astype(jnp.bfloat16)
    value_heads = projected_qkv[..., 2 * model_width :].astype(jnp.bfloat16)
    queries = queries.reshape(win_count, places, head_count, head_size)
    key_heads = key_heads.reshape(win_count, places, head_count, head_size)
    value_heads = value_heads.reshape(win_count, places, head_count, head_size)
    scores = (
        jnp.einsum("wihd,wjhd->whij", queries, key_heads, preferred_element_type=jnp.float32)
        + pos_bias[None]
    )
    row_peak = jnp.max(scores, axis=-1, keepdims=True)
    exp_scores = jnp.exp(scores - row_peak)
    weights_bf = (exp_scores / jnp.sum(exp_scores, axis=-1, keepdims=True)).astype(jnp.bfloat16)
    context = jnp.einsum(
        "whij,wjhd->wihd", weights_bf, value_heads, preferred_element_type=jnp.float32
    )
    context = context.astype(jnp.bfloat16).reshape(win_count, places, model_width)
    attended = windows.astype(jnp.float32) + jnp.dot(
        context, w_out, preferred_element_type=jnp.float32
    )
    return attended.astype(jnp.bfloat16)


def feed_forward(tokens_in, ffn_gain, ffn_shift, w_up, b_up, w_down, b_down):
    normed = layer_norm(tokens_in.astype(jnp.float32), ffn_gain, ffn_shift).astype(jnp.bfloat16)
    hidden = gelu_tanh(jnp.dot(normed, w_up, preferred_element_type=jnp.float32) + b_up).astype(
        jnp.bfloat16
    )
    result = (
        tokens_in.astype(jnp.float32)
        + jnp.dot(hidden, w_down, preferred_element_type=jnp.float32)
        + b_down
    )
    return result.astype(jnp.bfloat16)


def local(
    image,
    bn_gain,
    bn_shift,
    w_expand,
    b_expand,
    w_depth,
    b_depth,
    w_project,
    b_project,
    attn_gain,
    attn_shift,
    w_qkv,
    w_out,
    rel_table,
    ffn_gain,
    ffn_shift,
    w_up,
    b_up,
    w_down,
    b_down,
):
    tile_rows = image.shape[0]
    tile_cols = image.shape[1]
    channels = image.shape[2]
    strips = lax.axis_size("strip")
    tile_count = lax.axis_size("tile")
    framed_in = padded(image, (("tile", 1), ("strip", 0)), 1)
    expanded = expand_tokens(framed_in, bn_gain, bn_shift, w_expand, b_expand)
    row_global = (
        lax.axis_index("strip") * tile_rows - 1 + jnp.arange(tile_rows + 2, dtype=jnp.int32)
    )
    col_global = lax.axis_index("tile") * tile_cols - 1 + jnp.arange(tile_cols + 2, dtype=jnp.int32)
    row_ok = (row_global >= 0) & (row_global < tile_rows * strips)
    col_ok = (col_global >= 0) & (col_global < tile_cols * tile_count)
    keep_mask = row_ok[:, None, None] & col_ok[None, :, None]
    framed = jnp.where(keep_mask, expanded, jnp.zeros((), jnp.bfloat16))
    hidden = depthwise(framed, w_depth, b_depth)
    projected = jnp.dot(hidden, w_project, preferred_element_type=jnp.float32) + b_project
    section_one = (image.astype(jnp.float32) + projected).astype(jnp.bfloat16)
    grid_rows = GRID // strips
    across = tile_rows // grid_rows
    col_groups = tile_count // GRID
    flattened = section_one.reshape(grid_rows, across * tile_cols, channels)
    pos_bias = position_bias(rel_table)
    arrived = lax.all_to_all(
        lax.all_to_all(flattened, "tile", split_axis=1, concat_axis=0, tiled=True),
        "strip",
        split_axis=1,
        concat_axis=0,
        tiled=True,
    )
    per_piece = arrived.shape[1]
    windows = arrived.reshape(strips, GRID, col_groups, grid_rows, per_piece, channels).transpose(
        2, 4, 0, 3, 1, 5
    )
    windows = windows.reshape(col_groups * per_piece, GRID * GRID, channels)
    section_two = grid_attention(windows, attn_gain, attn_shift, w_qkv, w_out, pos_bias)
    sectioned = section_two.reshape(
        col_groups, per_piece, strips, grid_rows, GRID, channels
    ).transpose(2, 4, 0, 3, 1, 5)
    sectioned = sectioned.reshape(strips * GRID * col_groups * grid_rows, per_piece, channels)
    returned = lax.all_to_all(
        lax.all_to_all(sectioned, "strip", split_axis=0, concat_axis=1, tiled=True),
        "tile",
        split_axis=0,
        concat_axis=1,
        tiled=True,
    )
    section_image = returned.reshape(tile_rows, tile_cols, channels)
    return feed_forward(section_image, ffn_gain, ffn_shift, w_up, b_up, w_down, b_down)


def solution(mesh):
    return jax.shard_map(
        local,
        mesh=mesh,
        in_specs=(
            P(("group", "strip"), "tile", None),
            P(),
            P(),
            P(),
            P(),
            P(),
            P(),
            P(),
            P(),
            P(),
            P(),
            P(),
            P(),
            P(),
            P(),
            P(),
            P(),
            P(),
            P(),
            P(),
        ),
        out_specs=P(("group", "strip"), "tile", None),
        check_vma=False,
    )
```

profile of v0, /device:TPU:0, one launch (start us, length us, event | category | flops | bytes accessed | tf_op | source)
XLA Modules:
  0.0 97.8 jit_solution(2765681559433240991)
XLA Ops:
  0.0 1.1 %fusion.96 = (bf16[32,1,256]{2,1,0:T(2,128)(2,1)S(1)}, bf16[32,1,256]{2,1,0:T(2,128)(2,1)S(1)}) fusion(bf16[32,32,256]{2,1,0:T(8,128)(2,1)} %param.20), kind=kLoop, calls=%fused_computation.118 | loop fusion | bytes 65536 | tf_op jit(solution)/shard_map/slice | solution.py:17
  1.1 4.9 %collective-permute-start = (bf16[32,1,256]{2,1,0:T(2,128)(2,1)S(1)}, bf16[32,1,256]{2,1,0:T(2,128)(2,1)S(1)}, u32[]{:S(2)}, u32[]{:S(2)}) collective-permute-start(bf16[32,1,256]{2,1,0:T(2,128)(2,1)S(1)} %get-tuple-element.9), channel_id=1, source_target_pairs={{0,2},{2,4},{4,6},{6,8},{8,10},{10,12},{12,14},{1,3},{3,5},{5,7},{... | collective-permute-start | bytes 49160 | tf_op jit(solution)/shard_map/ppermute | solution.py:19
  6.0 1.3 %collective-permute-start.1 = (bf16[32,1,256]{2,1,0:T(2,128)(2,1)S(1)}, bf16[32,1,256]{2,1,0:T(2,128)(2,1)S(1)}, u32[]{:S(2)}, u32[]{:S(2)}) collective-permute-start(bf16[32,1,256]{2,1,0:T(2,128)(2,1)S(1)} %get-tuple-element.10), channel_id=1, source_target_pairs={{2,0},{4,2},{6,4},{8,6},{10,8},{12,10},{14,12},{3,1},{5,3},{7,5},{... | collective-permute-start | bytes 49160 | tf_op jit(solution)/shard_map/ppermute | solution.py:20
  7.3 1.1 %fusion.97 = (f32[1,1024]{1,0:T(1,128)S(1)}, f32[1,1024]{1,0:T(1,128)S(1)}, f32[1,1024]{1,0:T(1,128)S(1)}, f32[1,1024]{1,0:T(1,128)S(1)}, f32[1,1024]{1,0:T(1,12...) fusion(f32[9,1024]{1,0:T(8,128)} %param.25), kind=kLoop, calls=%fused_computation.119 | loop fusion | bytes 73728 | tf_op jit(solution)/shard_map/slice | solution.py:49
  8.4 3.4 %collective-permute-done.1 = bf16[32,1,256]{2,1,0:T(2,128)(2,1)S(1)} collective-permute-done((bf16[32,1,256]{2,1,0:T(2,128)(2,1)S(1)}, bf16[32,1,256]{2,1,0:T(2,128)(2,1)S(1)}, u32[]{:S(2)}, u32[]{:S(2)}) %collective-permute-start.1) | collective-permute-done | bytes 16416 | tf_op jit(solution)/shard_map/ppermute | solution.py:20
  11.8 0.8 pad_maximum_fusion.2
  12.5 1.3 %collective-permute-start.2 = (bf16[1,34,256]{2,1,0:T(8,128)(2,1)S(1)}, bf16[1,34,256]{2,1,0:T(8,128)(2,1)S(1)}, u32[]{:S(2)}, u32[]{:S(2)}) collective-permute-start(bf16[1,34,256]{2,1,0:T(8,128)(2,1)S(1)} %get-tuple-element.7), channel_id=1, source_target_pairs={{0,1},{2,3},{4,5},{6,7},{8,9},{10,11},{12,13},{14,15},{16,17},{18,... | collective-permute-start | bytes 52232 | tf_op jit(solution)/shard_map/ppermute | solution.py:19
  13.8 1.3 %collective-permute-start.3 = (bf16[1,34,256]{2,1,0:T(8,128)(2,1)S(1)}, bf16[1,34,256]{2,1,0:T(8,128)(2,1)S(1)}, u32[]{:S(2)}, u32[]{:S(2)}) collective-permute-start(bf16[1,34,256]{2,1,0:T(8,128)(2,1)S(1)} %get-tuple-element.8), channel_id=1, source_target_pairs={{1,0},{3,2},{5,4},{7,6},{9,8},{11,10},{13,12},{15,14},{17,16},{19,... | collective-permute-start | bytes 52232 | tf_op jit(solution)/shard_map/ppermute | solution.py:20
  15.2 1.7 %collective-permute-done.3 = bf16[1,34,256]{2,1,0:T(8,128)(2,1)S(1)} collective-permute-done((bf16[1,34,256]{2,1,0:T(8,128)(2,1)S(1)}, bf16[1,34,256]{2,1,0:T(8,128)(2,1)S(1)}, u32[]{:S(2)}, u32[]{:S(2)}) %collective-permute-start.3) | collective-permute-done | bytes 17440 | tf_op jit(solution)/shard_map/ppermute | solution.py:20
  16.9 3.7 %fusion.28 = bf16[34,34,1024]{2,1,0:T(8,128)(2,1)S(1)} fusion(f32[1024]{0:T(1024)} %param.24, pred[34,34]{1,0:T(8,128)(4,1)S(1)} %broadcast_and_fusion, bf16[1,34,256]{2,1,0:T(8,128)(2,1)S(1)} %collective-permute-done.3, bf16[32,1,256]{2,1,0:T(2,128)(2,1)S(1)} %collective-permute-done.1, bf16[32,32,256]{2,1,0:T(8,128)(2,1)} %param.20, ...), kind=kOutput, calls=%fused_computation.34 | convolution fusion | flops 622945280 | bytes 3490948 | tf_op jit(solution)/shard_map/dot_general | solution.py:37
  20.6 6.3 %fusion.46 = bf16[32,32,256]{2,1,0:T(8,128)(2,1)S(1)} fusion(bf16[34,34,1024]{2,1,0:T(8,128)(2,1)S(1)} %fusion.28, f32[1024]{0:T(1024)S(1)} %bitcast.121, f32[1024]{0:T(1024)S(1)} %bitcast.122, f32[1024]{0:T(1024)S(1)} %bitcast.115, f32[1024]{0:T(1024)S(1)} %bitcast.116, f32[1024]{0:T(1024)S(1)} %bitcast.117, f32[1024]{0:T(1024)S(1)} %bitcast.118, ...), kind=kOutput, calls=%fused_computation.49 | convolution fusion | flops 575668224 | bytes 20489216 | tf_op jit(solution)/shard_map/dot_general | solution.py:152
  26.9 1.2 %copy.124 = bf16[4,256,256]{2,0,1:T(4,128)(2,1)} copy(bf16[4,256,256]{2,1,0:T(8,128)(2,1)S(1)} %bitcast.111) | data formatting | bytes 1048576 | tf_op jit(solution)/shard_map/reshape | solution.py:157
  28.2 5.7 %all-to-all-start = ((bf16[4,256,256]{2,0,1:T(4,128)(2,1)}), bf16[4,256,256]{2,0,1:T(4,128)(2,1)S(1)}, u32[]{:S(2)}, u32[]{:S(2)}) async-start(bf16[4,256,256]{2,0,1:T(4,128)(2,1)} %copy.124), calls=%async_computation | async-start | bytes 1048576 | tf_op jit(solution)/shard_map/all_to_all | solution.py:160
  34.1 2.6 %convolution_bitcast_fusion = f32[8,4096]{1,0:T(8,128)S(1)} fusion(f32[8,225]{1,0:T(8,128)S(1)} %copy-done.11, s32[4096]{0:T(1024)S(1)} %add.259), kind=kOutput, calls=%fused_computation.12 | convolution fusion | flops 89395200 | bytes 154656 | tf_op jit(solution)/shard_map/dot_general | solution.py:64
  36.9 11.8 %all-to-all-done = bf16[4,256,256]{2,0,1:T(4,128)(2,1)S(1)} async-done(((bf16[4,256,256]{2,0,1:T(4,128)(2,1)}), bf16[4,256,256]{2,0,1:T(4,128)(2,1)S(1)}, u32[]{:S(2)}, u32[]{:S(2)}) %all-to-all-start) | async-done | bytes 524320 | tf_op jit(solution)/shard_map/all_to_all | solution.py:160
  48.9 0.3 copy.127
  49.2 4.2 %all_to_all.57 = bf16[32,32,256]{2,0,1:T(8,128)(2,1)S(1)} all-to-all(bf16[32,32,256]{2,0,1:T(8,128)(2,1)S(1)} %copy.127), channel_id=1, replica_groups=mesh['group'=2,'tile'=8,'strip'=2] {'strip'}, dimensions={1} | all-to-all | bytes 1048576 | tf_op jit(solution)/shard_map/all_to_all | solution.py:159
  53.9 0.6 copy.130
  54.8 0.4 multiply_reduce_fusion.1
  55.4 2.4 %fusion.98 = (bf16[16,64,768]{2,1,0:T(8,128)(2,1)S(1)}, f32[16,64,768]{2,1,0:T(8,128)}) fusion(bf16[256,768]{1,0:T(8,128)(2,1)S(1)} %copy-done.2, f32[16,64,256]{2,1,0:T(8,128)S(1)} %bitcast.95, f32[256]{0:T(256)S(1)} %copy-done.6, f32[256]{0:T(256)S(1)} %copy-done.7, f32[16,64]{1,0:T(8,128)S(1)} %copy.135, f32[16,64]{1,0:T(8,128)S(1)} %copy.132), kind=kOutput, calls=%fused_computation.120 | convolution fusion | flops 404750336 | bytes 6170624 | tf_op jit(solution)/shard_map/dot_general | solution.py:77
  57.9 1.3 %copy.138 = bf16[16,64,256]{1,2,0:T(8,128)(2,1)} copy(bf16[16,64,256]{2,1,0:T(8,128)(2,1)S(1)} %get-tuple-element.5) | data formatting | bytes 1048576 | tf_op jit(solution)/shard_map/slice | solution.py:79
  59.2 1.3 %fusion.49 = bf16[16,64,256]{2,1,0:T(8,128)(2,1)S(1)} fusion(f32[16,64,768]{2,1,0:T(8,128)} %get-tuple-element.23), kind=kLoop, calls=%fused_computation.51 | loop fusion | flops 524288 | bytes 1572864 | tf_op jit(solution)/shard_map/convert_element_type | solution.py:78
  60.5 1.4 %copy.137 = bf16[16,64,256]{1,2,0:T(8,128)(2,1)} copy(bf16[16,64,256]{2,1,0:T(8,128)(2,1)S(1)} %fusion.49) | data formatting | bytes 1048576 | tf_op jit(solution)/shard_map/convert_element_type | solution.py:78
  61.9 0.5 copy.136
  62.4 5.1 %fusion.99 = (f32[16,8,64]{2,1,0:T(8,128)S(1)}, f32[16,8,64,64]{2,3,1,0:T(8,128)}) fusion(f32[8,64,64]{1,2,0:T(8,128)S(1)} %copy.139, bf16[16,64,8,32]{1,3,2,0:T(8,128)(2,1)} %bitcast.108, bf16[16,64,8,32]{1,3,2,0:T(8,128)(2,1)} %bitcast.107), kind=kOutput, calls=%fused_computation.121 | convolution fusion | flops 35127360 | bytes 3309568 | tf_op jit(solution)/shard_map/sub | solution.py:89
  67.5 2.9 %fusion.34 = bf16[16,8,32,64]{3,2,1,0:T(8,128)(2,1)S(1)} fusion(bf16[16,64,8,32]{1,3,2,0:T(8,128)(2,1)S(1)} %bitcast.109, f32[16,8,64,64]{2,3,1,0:T(8,128)} %get-tuple-element.25, f32[16,8,64]{2,1,0:T(8,128)S(1)} %get-tuple-element.24), kind=kOutput, calls=%fused_computation.39 | convolution fusion | flops 34865152 | bytes 3178496 | tf_op jit(solution)/shard_map/whij,wjhd->wihd/dot_general | solution.py:91
  70.4 0.5 fusion.45
  71.2 4.2 %all_to_all.58 = bf16[64,16,256]{2,1,0:T(8,128)(2,1)S(1)} all-to-all(bf16[64,16,256]{2,1,0:T(8,128)(2,1)S(1)} %bitcast.103), channel_id=1, replica_groups=mesh['group'=2,'tile'=8,'strip'=2] {'strip'}, dimensions={0} | all-to-all | bytes 1048576 | tf_op jit(solution)/shard_map/all_to_all | solution.py:177
  75.5 18.3 %all_to_all.59 = bf16[32,32,256]{2,1,0:T(8,128)(2,1)S(1)} all-to-all(bf16[32,32,256]{2,1,0:T(8,128)(2,1)S(1)} %bitcast.105), channel_id=1, replica_groups=mesh['group'=2,'tile'=8,'strip'=2] {'tile'}, dimensions={0} | all-to-all | bytes 1048576 | tf_op jit(solution)/shard_map/all_to_all | solution.py:176
  94.1 0.4 multiply_reduce_fusion
  94.7 0.3 fusion.53
  95.1 2.6 %fusion.44 = bf16[32,32,256]{2,1,0:T(8,128)(2,1)} fusion(f32[32,32,256]{2,1,0:T(8,128)S(1)} %bitcast.99, bf16[32,32,256]{2,1,0:T(8,128)(2,1)S(1)} %fusion.53, f32[1024]{0:T(1024)S(1)} %copy-done.13, bf16[1024,256]{1,0:T(8,128)(2,1)S(1)} %copy-done.9, bf16[256,1024]{1,0:T(8,128)(2,1)S(1)} %copy-done.10, f32[256]{0:T(256)S(1)} %copy-done.15), kind=kOutput, calls=%fused_computation.47 | convolution fusion | flops 1085014016 | bytes 3150848 | tf_op jit(solution)/shard_map/dot_general | solution.py:108
  (61 shorter events, 2.5 us)
Async XLA Ops:
  0.0 16.9 %copy-start = (bf16[256,1024]{1,0:T(8,128)(2,1)S(1)}, bf16[256,1024]{1,0:T(8,128)(2,1)}, u32[]{:S(2)}) copy-start(bf16[256,1024]{1,0:T(8,128)(2,1)} %param.23) | copy-start | bytes 1572868
  1.1 7.3 %collective-permute-start = (bf16[32,1,256]{2,1,0:T(2,128)(2,1)S(1)}, bf16[32,1,256]{2,1,0:T(2,128)(2,1)S(1)}, u32[]{:S(2)}, u32[]{:S(2)}) collective-permute-start(bf16[32,1,256]{2,1,0:T(2,128)(2,1)S(1)} %get-tuple-element.9), channel_id=1, source_target_pairs={{0,2},{2,4},{4,6},{6,8},{8,10},{10,12},{12,14},{1,3},{3,5},{5,7},{... | collective-permute-start | bytes 49160 | tf_op jit(solution)/shard_map/ppermute | solution.py:19
  6.0 5.8 %collective-permute-start.1 = (bf16[32,1,256]{2,1,0:T(2,128)(2,1)S(1)}, bf16[32,1,256]{2,1,0:T(2,128)(2,1)S(1)}, u32[]{:S(2)}, u32[]{:S(2)}) collective-permute-start(bf16[32,1,256]{2,1,0:T(2,128)(2,1)S(1)} %get-tuple-element.10), channel_id=1, source_target_pairs={{2,0},{4,2},{6,4},{8,6},{10,8},{12,10},{14,12},{3,1},{5,3},{7,5},{... | collective-permute-start | bytes 49160 | tf_op jit(solution)/shard_map/ppermute | solution.py:20
  12.5 2.7 %collective-permute-start.2 = (bf16[1,34,256]{2,1,0:T(8,128)(2,1)S(1)}, bf16[1,34,256]{2,1,0:T(8,128)(2,1)S(1)}, u32[]{:S(2)}, u32[]{:S(2)}) collective-permute-start(bf16[1,34,256]{2,1,0:T(8,128)(2,1)S(1)} %get-tuple-element.7), channel_id=1, source_target_pairs={{0,1},{2,3},{4,5},{6,7},{8,9},{10,11},{12,13},{14,15},{16,17},{18,... | collective-permute-start | bytes 52232 | tf_op jit(solution)/shard_map/ppermute | solution.py:19
  13.8 3.1 %collective-permute-start.3 = (bf16[1,34,256]{2,1,0:T(8,128)(2,1)S(1)}, bf16[1,34,256]{2,1,0:T(8,128)(2,1)S(1)}, u32[]{:S(2)}, u32[]{:S(2)}) collective-permute-start(bf16[1,34,256]{2,1,0:T(8,128)(2,1)S(1)} %get-tuple-element.8), channel_id=1, source_target_pairs={{1,0},{3,2},{5,4},{7,6},{9,8},{11,10},{13,12},{15,14},{17,16},{19,... | collective-permute-start | bytes 52232 | tf_op jit(solution)/shard_map/ppermute | solution.py:20
  15.2 5.4 %copy-start.1 = (bf16[32,32,256]{2,1,0:T(8,128)(2,1)S(1)}, bf16[32,32,256]{2,1,0:T(8,128)(2,1)}, u32[]{:S(2)}) copy-start(bf16[32,32,256]{2,1,0:T(8,128)(2,1)} %param.20) | copy-start | bytes 1572868
  15.2 5.4 %copy-start.8 = (bf16[1024,256]{1,0:T(8,128)(2,1)S(1)}, bf16[1024,256]{1,0:T(8,128)(2,1)}, u32[]{:S(2)}) copy-start(bf16[1024,256]{1,0:T(8,128)(2,1)} %param.27) | copy-start | bytes 1572868
  15.2 5.4 %copy-start.12 = (f32[1024]{0:T(1024)S(1)}, f32[1024]{0:T(1024)}, u32[]{:S(2)}) copy-start(f32[1024]{0:T(1024)} %param.26) | copy-start | bytes 12292
  15.2 5.4 %copy-start.14 = (f32[256]{0:T(256)S(1)}, f32[256]{0:T(256)}, u32[]{:S(2)}) copy-start(f32[256]{0:T(256)} %param.28) | copy-start | bytes 3076
  20.6 13.5 %copy-start.11 = (f32[8,225]{1,0:T(8,128)S(1)}, f32[8,225]{1,0:T(8,128)}, u32[]{:S(2)}) copy-start(f32[8,225]{1,0:T(8,128)} %param.33) | copy-start | bytes 21604
  28.2 20.6 %all-to-all-start = ((bf16[4,256,256]{2,0,1:T(4,128)(2,1)}), bf16[4,256,256]{2,0,1:T(4,128)(2,1)S(1)}, u32[]{:S(2)}, u32[]{:S(2)}) async-start(bf16[4,256,256]{2,0,1:T(4,128)(2,1)} %copy.124), calls=%async_computation | async-start | bytes 1048576 | tf_op jit(solution)/shard_map/all_to_all | solution.py:160
  53.6 1.7 %copy-start.2 = (bf16[256,768]{1,0:T(8,128)(2,1)S(1)}, bf16[256,768]{1,0:T(8,128)(2,1)}, u32[]{:S(2)}) copy-start(bf16[256,768]{1,0:T(8,128)(2,1)} %param.31) | copy-start | bytes 1179652
  53.6 1.7 %copy-start.6 = (f32[256]{0:T(256)S(1)}, f32[256]{0:T(256)}, u32[]{:S(2)}) copy-start(f32[256]{0:T(256)} %param.30) | copy-start | bytes 3076
  53.6 1.7 %copy-start.7 = (f32[256]{0:T(256)S(1)}, f32[256]{0:T(256)}, u32[]{:S(2)}) copy-start(f32[256]{0:T(256)} %param.29) | copy-start | bytes 3076
  67.5 2.9 %copy-start.3 = (bf16[256,256]{1,0:T(8,128)(2,1)S(1)}, bf16[256,256]{1,0:T(8,128)(2,1)}, u32[]{:S(2)}) copy-start(bf16[256,256]{1,0:T(8,128)(2,1)} %param.32) | copy-start | bytes 393220
  71.2 23.5 %copy-start.4 = (f32[256]{0:T(256)S(1)}, f32[256]{0:T(256)}, u32[]{:S(2)}) copy-start(f32[256]{0:T(256)} %param.35) | copy-start | bytes 3076
  71.2 23.5 %copy-start.5 = (f32[256]{0:T(256)S(1)}, f32[256]{0:T(256)}, u32[]{:S(2)}) copy-start(f32[256]{0:T(256)} %param.34) | copy-start | bytes 3076
  75.4 19.7 %copy-start.9 = (bf16[1024,256]{1,0:T(8,128)(2,1)S(1)}, bf16[1024,256]{1,0:T(8,128)(2,1)}, u32[]{:S(2)}) copy-start(bf16[1024,256]{1,0:T(8,128)(2,1)} %param.38) | copy-start | bytes 1572868
  75.4 19.7 %copy-start.10 = (bf16[256,1024]{1,0:T(8,128)(2,1)S(1)}, bf16[256,1024]{1,0:T(8,128)(2,1)}, u32[]{:S(2)}) copy-start(bf16[256,1024]{1,0:T(8,128)(2,1)} %param.36) | copy-start | bytes 1572868
  75.4 19.7 %copy-start.13 = (f32[1024]{0:T(1024)S(1)}, f32[1024]{0:T(1024)}, u32[]{:S(2)}) copy-start(f32[1024]{0:T(1024)} %param.37) | copy-start | bytes 12292
  75.4 19.7 %copy-start.15 = (f32[256]{0:T(256)S(1)}, f32[256]{0:T(256)}, u32[]{:S(2)}) copy-start(f32[256]{0:T(256)} %param.39) | copy-start | bytes 3076
where the time goes:
time: 98.4 us; the launch traced here: 97.8 us
  blocking collectives  26.7 us (27%)
  matrix products  26.1 us (27%)
  waiting for transfers between devices  16.9 us (17%)
  starting transfers between devices  14.5 us (15%)
  local copies, waits for them, and re-layouts  9.03 us (9%)
  other arithmetic  4.18 us (4%)
    all_to_all x1, blocking collectives, local(): lax.all_to_all(lax.all_to_all(sectioned, 'strip', split_axis=0, concat_ax...  18.3 us
    all_to_all x1, waiting for transfers between devices, local(): lax.all_to_all(flattened, 'tile', split_axis=1, concat_axis=0, tiled=True)  11.8 us
    dot_general x1, matrix products, local(): jnp.dot(hidden, w_project, preferred_element_type=jnp.float32) + b_project  6.31 us
    ppermute x2, starting transfers between devices, padded(): before = lax.ppermute(last, axis, up)  6.16 us
    all_to_all x1, starting transfers between devices, local(): lax.all_to_all(flattened, 'tile', split_axis=1, concat_axis=0, tiled=True)  5.75 us
    sub x1, matrix products, grid_attention(): exp_scores = jnp.exp(scores - row_peak)  5.13 us
    ppermute x2, waiting for transfers between devices, padded(): after = lax.ppermute(initial, axis, down)  5.05 us
    all_to_all x1, blocking collectives, local(): lax.all_to_all(lax.all_to_all(flattened, 'tile', split_axis=1, concat_axi...  4.15 us
  transfers between devices with their start and end apart: 5, of which 3 were waited for; matrix products, arithmetic and copies ran while one was open for 4% of the time, Pallas kernels for 0%

commit v1 on v0

v1 whole, which is shorter than its diff:
```python
import functools

import jax
import jax.numpy as jnp
from jax import lax
from jax.experimental import pallas as pl
from jax.experimental.pallas import tpu as pltpu
from jax.sharding import PartitionSpec as P

GRID = 8
EPSILON = 1e-05
MESH = pl.DeviceIdType.MESH


def padded(value, sides, width):
    for axis, dim in sides:
        devices, length = (lax.axis_size(axis), value.shape[dim])
        up = [(i, (i + 1) % devices) for i in range(devices - 1)]
        down = [(j, i) for i, j in up]
        last = lax.slice_in_dim(value, length - width, length, axis=dim)
        initial = lax.slice_in_dim(value, 0, width, axis=dim)
        before = lax.ppermute(last, axis, up)
        after = lax.ppermute(initial, axis, down)
        value = jnp.concatenate([before, value, after], axis=dim)
    return value


def gelu_tanh(inputs):
    return jax.nn.gelu(inputs, approximate=True)


def layer_norm(inputs, norm_gain, norm_shift):
    center = jnp.mean(inputs, axis=-1, keepdims=True)
    spread = jnp.mean(jnp.square(inputs - center), axis=-1, keepdims=True)
    return (inputs - center) * lax.rsqrt(spread + EPSILON) * norm_gain + norm_shift


def expand_tokens(pixels, bn_gain, bn_shift, w_expand, b_expand):
    normed = (pixels.astype(jnp.float32) * bn_gain + bn_shift).astype(jnp.bfloat16)
    pre_act = jnp.dot(normed, w_expand, preferred_element_type=jnp.float32) + b_expand
    return gelu_tanh(pre_act).astype(jnp.bfloat16)


def depthwise(framed, w_depth, b_depth):
    out_rows = framed.shape[0] - 2
    out_cols = framed.shape[1] - 2
    accum_sum = jnp.zeros((out_rows, out_cols, framed.shape[2]), jnp.float32) + b_depth
    for row_step in range(3):
        for col_step in range(3):
            window_part = framed[row_step : row_step + out_rows, col_step : col_step + out_cols]
            accum_sum = (
                accum_sum + window_part.astype(jnp.float32) * w_depth[row_step * 3 + col_step]
            )
    return gelu_tanh(accum_sum).astype(jnp.bfloat16)


def place_bias(rel_table, piece):
    heads = rel_table.shape[0]
    side = 2 * GRID - 1
    table = rel_table.reshape(heads, side, side)
    by_row = jnp.stack(
        [table[:, GRID - 1 - k : 2 * GRID - 1 - k, :] for k in range(GRID)]
    )
    by_col = jnp.stack(
        [by_row[..., GRID - 1 - k : 2 * GRID - 1 - k] for k in range(GRID)], axis=1
    )
    rows = piece // GRID
    by_col = by_col.reshape(GRID * GRID, heads, GRID // rows, rows * GRID)
    return by_col.transpose(2, 0, 1, 3).reshape(GRID // rows, GRID * GRID, heads * piece)


def dot(a, b):
    return jnp.dot(a, b, preferred_element_type=jnp.float32)


def back_kernel(
    strips,
    col_groups,
    head_count,
    sec_ref,
    ag_ref,
    as_ref,
    wqkv_ref,
    wout_ref,
    bias_ref,
    fg_ref,
    fs_ref,
    wup_ref,
    bup_ref,
    wdown_ref,
    bdown_ref,
    out_ref,
    arr,
    q_s,
    k_s,
    v_s,
    ctx_s,
    outb,
    sec2,
    send1,
    recv1,
    send2,
    recv2,
):
    grid_rows, _, cols, chans = sec_ref.shape
    part = cols // strips
    piece = ctx_s.shape[1]
    blocks = GRID * GRID // piece
    per_block = piece // GRID
    head_size = chans // head_count
    me_s = lax.axis_index("strip")
    tile = lax.axis_index("tile")
    me_k = tile // col_groups
    within = tile % col_groups
    peers = strips * GRID

    def device(s, k):
        return {"strip": s, "tile": k * col_groups + within}

    def is_me(s, k):
        return jnp.logical_and(s == me_s, k == me_k)

    barrier = pltpu.get_barrier_semaphore()
    for m in range(1, peers):
        s, k = (me_s + m // GRID) % strips, (me_k + m) % GRID
        pl.semaphore_signal(barrier, inc=1, device_id=device(s, k), device_id_type=MESH)
    pl.semaphore_wait(barrier, peers - 1)

    def first_copy(m):
        s, k = (me_s + m // GRID) % strips, (me_k + m) % GRID
        src = sec_ref.at[:, k, pl.ds(part * s, part)]
        dst = arr.at[pl.ds(grid_rows * me_s, grid_rows), me_k]
        if m == 0:
            return pltpu.make_async_copy(src, dst, recv1.at[me_s, me_k])
        return pltpu.make_async_remote_copy(
            src, dst, send1.at[m], recv1.at[me_s, me_k], device_id=device(s, k), device_id_type=MESH
        )

    for m in list(range(1, peers)) + [0]:
        first_copy(m).start()

    def wait_first(s, k):
        piece_ref = arr.at[pl.ds(grid_rows * s, grid_rows), k]
        pltpu.make_async_copy(piece_ref, piece_ref, recv1.at[s, k]).wait()

    span = piece * part
    row_id = lax.broadcasted_iota(jnp.int32, (span, span), 0)
    col_id = lax.broadcasted_iota(jnp.int32, (span, span), 1)
    swap = jnp.where(col_id == (row_id % piece) * part + row_id // piece, 1.0, 0.0).astype(
        jnp.bfloat16
    )
    lane_head = lax.broadcasted_iota(jnp.int32, (head_count * piece, chans), 1) // head_size
    row_head = lax.broadcasted_iota(jnp.int32, (head_count * piece, chans), 0) // piece
    mask = jnp.where(lane_head == row_head, 1.0, 0.0)
    mask_bf = mask.astype(jnp.bfloat16)

    blocks_per_strip = blocks // strips
    for b in range(blocks):
        if b % blocks_per_strip == 0:
            for k in range(GRID):
                wait_first(b // blocks_per_strip, k)
        x = arr[per_block * b : per_block * (b + 1)].reshape(span, chans).astype(jnp.float32)
        normed = layer_norm(x, ag_ref[...], as_ref[...]).astype(jnp.bfloat16)
        normed = dot(swap, normed).astype(jnp.bfloat16)
        qkv = dot(normed, wqkv_ref[...])
        q = (qkv[:, :chans] * head_size ** (-0.5)).astype(jnp.bfloat16)
        q_s[b] = q.reshape(part, piece, chans)
        k_s[:, piece * b : piece * (b + 1), :] = (
            qkv[:, chans : 2 * chans].astype(jnp.bfloat16).reshape(part, piece, chans)
        )
        v_s[:, piece * b : piece * (b + 1), :] = (
            qkv[:, 2 * chans :].astype(jnp.bfloat16).reshape(part, piece, chans)
        )

    def back_copy(b, k):
        s = b // blocks_per_strip
        half = b % blocks_per_strip
        src = outb.at[pl.ds(per_block * b, per_block), k]
        dst = sec2.at[pl.ds(per_block * half, per_block), me_k, pl.ds(part * me_s, part)]
        remote = pltpu.make_async_remote_copy(
            src,
            dst,
            send2.at[b, k],
            recv2.at[half, me_s, me_k],
            device_id=device(s, k),
            device_id_type=MESH,
        )
        own = pltpu.make_async_copy(src, dst, recv2.at[half, me_s, me_k])
        return s, remote, own

    for b in range(blocks):
        for w in range(part):
            q16 = q_s[b, w]
            qbd = jnp.concatenate([q16] * head_count, axis=0) * mask_bf
            s = lax.dot_general(
                k_s[w], qbd, (((1,), (1,)), ((), ())), preferred_element_type=jnp.float32
            )
            s = s + bias_ref[b]
            e = jnp.exp(s - jnp.max(s, axis=0, keepdims=True))
            p = (e * (1.0 / jnp.sum(e, axis=0, keepdims=True))).astype(jnp.bfloat16)
            o = lax.dot_general(
                p, v_s[w], (((0,), (0,)), ((), ())), preferred_element_type=jnp.float32
            )
            o = (o * mask).reshape(head_count, piece, chans)
            ctx_s[w] = jnp.sum(o, axis=0).astype(jnp.bfloat16)
        ctx = dot(swap, ctx_s[...].reshape(span, chans)).astype(jnp.bfloat16)
        x = arr[per_block * b : per_block * (b + 1)].reshape(span, chans).astype(jnp.float32)
        attended = (x + dot(ctx, wout_ref[...])).astype(jnp.bfloat16)
        outb[per_block * b : per_block * (b + 1)] = attended.reshape(per_block, GRID, part, chans)
        for m in range(GRID):
            k = (me_k + m) % GRID
            s, remote, own = back_copy(b, k)

            @pl.when(jnp.logical_not(is_me(s, k)))
            def _():
                remote.start()

            @pl.when(is_me(s, k))
            def _():
                own.start()

    pairs = GRID // 2
    for m in range(pairs):
        pair = (me_k // 2 + m) % pairs
        for s in range(strips):
            for kk in range(2):
                k = 2 * pair + kk
                for half in range(blocks_per_strip):
                    ref = sec2.at[pl.ds(per_block * half, per_block), k, pl.ds(part * s, part)]
                    pltpu.make_async_copy(ref, ref, recv2.at[half, s, k]).wait()
        x = sec2[:, pl.ds(2 * pair, 2)].reshape(grid_rows * 2 * cols, chans).astype(jnp.float32)
        normed = layer_norm(x, fg_ref[...], fs_ref[...]).astype(jnp.bfloat16)
        hidden = gelu_tanh(dot(normed, wup_ref[...]) + bup_ref[...]).astype(jnp.bfloat16)
        res = x + dot(hidden, wdown_ref[...]) + bdown_ref[...]
        out_ref[:, pl.ds(2 * pair, 2)] = res.astype(jnp.bfloat16).reshape(
            grid_rows, 2, cols, chans
        )

    for m in range(1, peers):
        first_copy(m).wait_send()
    for b in range(blocks):
        for k in range(GRID):
            s, remote, own = back_copy(b, k)

            @pl.when(jnp.logical_not(is_me(s, k)))
            def _():
                remote.wait_send()


def local(
    image,
    bn_gain,
    bn_shift,
    w_expand,
    b_expand,
    w_depth,
    b_depth,
    w_project,
    b_project,
    attn_gain,
    attn_shift,
    w_qkv,
    w_out,
    rel_table,
    ffn_gain,
    ffn_shift,
    w_up,
    b_up,
    w_down,
    b_down,
):
    tile_rows, tile_cols, channels = image.shape
    strips = lax.axis_size("strip")
    tile_count = lax.axis_size("tile")
    framed_in = padded(image, (("tile", 1), ("strip", 0)), 1)
    expanded = expand_tokens(framed_in, bn_gain, bn_shift, w_expand, b_expand)
    row_global = (
        lax.axis_index("strip") * tile_rows - 1 + jnp.arange(tile_rows + 2, dtype=jnp.int32)
    )
    col_global = lax.axis_index("tile") * tile_cols - 1 + jnp.arange(tile_cols + 2, dtype=jnp.int32)
    row_ok = (row_global >= 0) & (row_global < tile_rows * strips)
    col_ok = (col_global >= 0) & (col_global < tile_cols * tile_count)
    keep_mask = row_ok[:, None, None] & col_ok[None, :, None]
    framed = jnp.where(keep_mask, expanded, jnp.zeros((), jnp.bfloat16))
    hidden = depthwise(framed, w_depth, b_depth)
    projected = jnp.dot(hidden, w_project, preferred_element_type=jnp.float32) + b_project
    section_one = (image.astype(jnp.float32) + projected).astype(jnp.bfloat16)

    grid_rows = GRID // strips
    across = tile_rows // grid_rows
    col_groups = tile_count // GRID
    heads = rel_table.shape[0]
    part = tile_cols // strips
    piece = part
    blocks = GRID * GRID // piece
    bias = place_bias(rel_table, piece)
    section = section_one.reshape(grid_rows, across, tile_cols, channels)
    bf = jnp.bfloat16
    vmem = pl.BlockSpec(memory_space=pltpu.VMEM)
    out = pl.pallas_call(
        functools.partial(back_kernel, strips, col_groups, heads),
        out_shape=jax.ShapeDtypeStruct(section.shape, bf),
        in_specs=[vmem] * 12,
        out_specs=vmem,
        scratch_shapes=[
            pltpu.VMEM((GRID, GRID, part, channels), bf),
            pltpu.VMEM((blocks, part, piece, channels), bf),
            pltpu.VMEM((part, GRID * GRID, channels), bf),
            pltpu.VMEM((part, GRID * GRID, channels), bf),
            pltpu.VMEM((part, piece, channels), bf),
            pltpu.VMEM((GRID, GRID, part, channels), bf),
            pltpu.VMEM((grid_rows, GRID, tile_cols, channels), bf),
            pltpu.SemaphoreType.DMA((strips * GRID,)),
            pltpu.SemaphoreType.DMA((strips, GRID)),
            pltpu.SemaphoreType.DMA((blocks, GRID)),
            pltpu.SemaphoreType.DMA((blocks // strips, strips, GRID)),
        ],
        compiler_params=pltpu.CompilerParams(collective_id=0, has_side_effects=True),
    )(
        section,
        attn_gain.reshape(1, -1),
        attn_shift.reshape(1, -1),
        w_qkv,
        w_out,
        bias,
        ffn_gain.reshape(1, -1),
        ffn_shift.reshape(1, -1),
        w_up,
        b_up.reshape(1, -1),
        w_down,
        b_down.reshape(1, -1),
    )
    return out.reshape(tile_rows, tile_cols, channels)


def solution(mesh):
    return jax.shard_map(
        local,
        mesh=mesh,
        in_specs=(P(("group", "strip"), "tile", None),) + (P(),) * 19,
        out_specs=P(("group", "strip"), "tile", None),
        check_vma=False,
    )
```

time: 98.4 us -> 74.4 us (0.76)
  the two profiles are of different devices: /device:TPU:0 before, /device:TPU:1 now
where the time goes in v1:
time: 74.4 us; the launch traced here: 74 us
  Pallas kernels  37 us (50%)
  local copies, waits for them, and re-layouts  15.3 us (21%)
  starting transfers between devices  10.7 us (14%)
  matrix products  10.7 us (14%)
    pallas_call x1, Pallas kernels, local(): pl.pallas_call(functools.partial(back_kernel, strips, col_groups, heads),...  37 us
    unnamed x29, local copies, waits for them, and re-layouts  7.89 us
    dot_general x1, matrix products, local(): jnp.dot(hidden, w_project, preferred_element_type=jnp.float32) + b_project  7.27 us
    ppermute x2, starting transfers between devices, padded(): after = lax.ppermute(initial, axis, down)  5.52 us
    ppermute x2, starting transfers between devices, padded(): before = lax.ppermute(last, axis, up)  5.23 us
    another operation x2, local copies, waits for them, and re-layouts, place_bias(): jnp.stack([by_row[..., GRID - 1 - k:2 * GRID - 1 - k] for k in range(GRID...  3.51 us
    dot_general x1, matrix products, expand_tokens(): jnp.dot(normed, w_expand, preferred_element_type=jnp.float32) + b_expand  3.44 us
  transfers between devices with their start and end apart: 4, of which 0 were waited for; matrix products, arithmetic and copies ran while one was open for 17% of the time, Pallas kernels for 0%

profile of v1, /device:TPU:1, one launch (start us, length us, event | category | flops | bytes accessed | tf_op | source)
XLA Modules:
  0.0 74.0 jit_solution(18258536967165699485)
XLA Ops:
  0.0 0.0 copy-start
  0.0 1.1 %fusion.54 = (bf16[32,1,256]{2,1,0:T(2,128)(2,1)S(1)}, bf16[32,1,256]{2,1,0:T(2,128)(2,1)S(1)}) fusion(bf16[32,32,256]{2,1,0:T(8,128)(2,1)} %param.20), kind=kLoop, calls=%fused_computation.80 | loop fusion | bytes 65536 | tf_op jit(solution)/shard_map/slice | solution.py:20
  1.1 3.9 %collective-permute-start = (bf16[32,1,256]{2,1,0:T(2,128)(2,1)S(1)}, bf16[32,1,256]{2,1,0:T(2,128)(2,1)S(1)}, u32[]{:S(2)}, u32[]{:S(2)}) collective-permute-start(bf16[32,1,256]{2,1,0:T(2,128)(2,1)S(1)} %get-tuple-element.7), channel_id=1, source_target_pairs={{0,2},{2,4},{4,6},{6,8},{8,10},{10,12},{12,14},{1,3},{3,5},{5,7},{... | collective-permute-start | bytes 49160 | tf_op jit(solution)/shard_map/ppermute | solution.py:22
  5.1 1.3 %collective-permute-start.1 = (bf16[32,1,256]{2,1,0:T(2,128)(2,1)S(1)}, bf16[32,1,256]{2,1,0:T(2,128)(2,1)S(1)}, u32[]{:S(2)}, u32[]{:S(2)}) collective-permute-start(bf16[32,1,256]{2,1,0:T(2,128)(2,1)S(1)} %get-tuple-element.8), channel_id=1, source_target_pairs={{2,0},{4,2},{6,4},{8,6},{10,8},{12,10},{14,12},{3,1},{5,3},{7,5},{... | collective-permute-start | bytes 49160 | tf_op jit(solution)/shard_map/ppermute | solution.py:23
  6.4 0.8 %reshape.96 = f32[8,15,15]{2,1,0:T(8,128)S(1)} reshape(f32[8,225]{1,0:T(8,128)} %param.33) | data formatting | bytes 14400 | tf_op jit(solution)/shard_map/reshape | solution.py:60
  7.3 0.8 %fusion.48 = f32[8,8,8,8,8]{4,3,2,0,1:T(8,128)} fusion(f32[8,8,8,15]{3,2,1,0:T(8,128)S(1)} %constant_dynamic-update-slice_fusion), kind=kLoop, calls=%fused_computation.52 | loop fusion | bytes 278528
  8.1 0.8 %fusion.47 = f32[8,8,8,8,8]{4,3,2,0,1:T(8,128)} fusion(f32[8,8,8,8,8]{4,3,2,0,1:T(8,128)} %fusion.48, f32[8,8,8,15]{3,2,1,0:T(8,128)S(1)} %constant_dynamic-update-slice_fusion), kind=kLoop, calls=%fused_computation.50 | loop fusion | bytes 278528
  9.0 0.9 %fusion.46 = f32[8,8,8,8,8]{4,3,2,0,1:T(8,128)} fusion(f32[8,8,8,8,8]{4,3,2,0,1:T(8,128)} %fusion.47, f32[8,8,8,15]{3,2,1,0:T(8,128)S(1)} %constant_dynamic-update-slice_fusion), kind=kLoop, calls=%fused_computation.48 | loop fusion | bytes 278528
  9.8 0.9 %fusion.45 = f32[8,8,8,8,8]{4,3,2,0,1:T(8,128)} fusion(f32[8,8,8,8,8]{4,3,2,0,1:T(8,128)} %fusion.46, f32[8,8,8,15]{3,2,1,0:T(8,128)S(1)} %constant_dynamic-update-slice_fusion), kind=kLoop, calls=%fused_computation.46 | loop fusion | bytes 278528
  10.7 0.9 %fusion.44 = f32[8,8,8,8,8]{4,3,2,0,1:T(8,128)} fusion(f32[8,8,8,8,8]{4,3,2,0,1:T(8,128)} %fusion.45, f32[8,8,8,15]{3,2,1,0:T(8,128)S(1)} %constant_dynamic-update-slice_fusion), kind=kLoop, calls=%fused_computation.44 | loop fusion | bytes 278528
  11.5 0.8 %fusion.43 = f32[8,8,8,8,8]{4,3,2,0,1:T(8,128)} fusion(f32[8,8,8,8,8]{4,3,2,0,1:T(8,128)} %fusion.44, f32[8,8,8,15]{3,2,1,0:T(8,128)S(1)} %constant_dynamic-update-slice_fusion), kind=kLoop, calls=%fused_computation.42 | loop fusion | bytes 278528
  12.4 0.9 %fusion.42 = f32[8,8,8,8,8]{4,3,2,0,1:T(8,128)} fusion(f32[8,8,8,8,8]{4,3,2,0,1:T(8,128)} %fusion.43, f32[8,8,8,15]{3,2,1,0:T(8,128)S(1)} %constant_dynamic-update-slice_fusion), kind=kLoop, calls=%fused_computation.40 | loop fusion | bytes 278528
  13.2 0.7 fusion.41
  14.0 0.0 copy-done.2
  14.0 0.6 fusion.55
  14.6 0.0 collective-permute-done
  14.6 0.0 collective-permute-done.1
  14.6 0.0 copy-done.1
  14.7 1.3 %collective-permute-start.2 = (bf16[1,34,256]{2,1,0:T(8,128)(2,1)S(1)}, bf16[1,34,256]{2,1,0:T(8,128)(2,1)}, u32[]{:S(2)}, u32[]{:S(2)}) collective-permute-start(bf16[1,34,256]{2,1,0:T(8,128)(2,1)S(1)} %get-tuple-element.5), channel_id=1, source_target_pairs={{0,1},{2,3},{4,5},{6,7},{8,9},{10,11},{12,13},{14,15},{16,17},{18,... | collective-permute-start | bytes 52232 | tf_op jit(solution)/shard_map/ppermute | solution.py:22
  16.0 4.2 %collective-permute-start.3 = (bf16[1,34,256]{2,1,0:T(8,128)(2,1)S(1)}, bf16[1,34,256]{2,1,0:T(8,128)(2,1)}, u32[]{:S(2)}, u32[]{:S(2)}) collective-permute-start(bf16[1,34,256]{2,1,0:T(8,128)(2,1)S(1)} %get-tuple-element.6), channel_id=1, source_target_pairs={{1,0},{3,2},{5,4},{7,6},{9,8},{11,10},{13,12},{15,14},{17,16},{19,... | collective-permute-start | bytes 52232 | tf_op jit(solution)/shard_map/ppermute | solution.py:23
  20.2 0.1 broadcast_and_fusion
  20.3 2.8 %copy.21 = f32[8,8,8,8,8]{1,0,4,3,2:T(8,128)S(1)} copy(f32[8,8,8,8,8]{4,3,2,0,1:T(8,128)} %fusion.41) | data formatting | bytes 262144 | tf_op jit(solution)/shard_map/stack | solution.py:64
  23.0 0.6 reshape.97
  23.6 0.8 %copy.23.bias_ref = f32[4,64,128]{2,1,0:T(8,128)} copy(f32[4,64,128]{1,2,0:T(8,128)S(1)} %bitcast.95) | data formatting | bytes 262144 | tf_op jit(solution)/shard_map/reshape | solution.py:69
  24.4 0.0 collective-permute-done.2
  24.4 0.0 collective-permute-done.3
  24.4 0.0 copy-done
  24.4 3.4 %fusion.16 = bf16[34,34,1024]{2,1,0:T(8,128)(2,1)S(1)} fusion(f32[1024]{0:T(1024)} %param.24, pred[34,34]{1,0:T(8,128)(4,1)S(1)} %broadcast_and_fusion, bf16[1,34,256]{2,1,0:T(8,128)(2,1)} %collective-permute-done.3, bf16[32,1,256]{2,1,0:T(2,128)(2,1)S(1)} %collective-permute-done.1, bf16[32,32,256]{2,1,0:T(8,128)(2,1)S(1)} %copy-done.1, ...), kind=kOutput, calls=%fused_computation.18 | convolution fusion | flops 622945280 | bytes 3490948 | tf_op jit(solution)/shard_map/dot_general | solution.py:40
  27.9 0.0 copy-done.3
  27.9 7.3 %fusion.25 = bf16[32,32,256]{2,1,0:T(8,128)(2,1)} fusion(bf16[34,34,1024]{2,1,0:T(8,128)(2,1)S(1)} %fusion.16, f32[1024]{0:T(1024)S(1)} %bitcast.105, f32[1024]{0:T(1024)S(1)} %bitcast.106, f32[1024]{0:T(1024)S(1)} %bitcast.99, f32[1024]{0:T(1024)S(1)} %bitcast.100, f32[1024]{0:T(1024)S(1)} %bitcast.101, f32[1024]{0:T(1024)S(1)} %bitcast.102, ...), kind=kOutput, calls=%fused_computation.23 | convolution fusion | flops 575668224 | bytes 20489216 | tf_op jit(solution)/shard_map/dot_general | solution.py:286
  35.2 37.0 %shard_map.190 = bf16[4,8,32,256]{3,2,1,0:T(8,128)(2,1)} custom-call(bf16[4,8,32,256]{3,2,1,0:T(8,128)(2,1)} %bitcast.96, f32[1,256]{1,0:T(1,128)} %bitcast.107, f32[1,256]{1,0:T(1,128)} %bitcast.108, bf16[256,768]{1,0:T(8,128)(2,1)} %wqkv_ref.1, bf16[256,256]{1,0:T(8,128)(2,1)} %wout_ref.1, f32[4,64,128]{2,1,0:T(8,128)} %copy.23.bias_ref, ...), custom_call_target="tpu_custom_call" | custom-call | tf_op jit(solution)/shard_map/pallas_call | solution.py:300
  72.1 1.9 %copy.39 = bf16[32,32,256]{2,1,0:T(8,128)(2,1)} copy(bf16[32,32,256]{2,1,0:T(8,128)(2,1)} %bitcast.93) | data formatting | bytes 1048576
  (20 shorter events, 0.1 us)
Async XLA Ops:
  0.0 24.4 %copy-start = (bf16[256,1024]{1,0:T(8,128)(2,1)S(1)}, bf16[256,1024]{1,0:T(8,128)(2,1)}, u32[]{:S(2)}) copy-start(bf16[256,1024]{1,0:T(8,128)(2,1)} %param.23) | copy-start | bytes 1572868
  0.0 14.6 %copy-start.1 = (bf16[32,32,256]{2,1,0:T(8,128)(2,1)S(1)}, bf16[32,32,256]{2,1,0:T(8,128)(2,1)}, u32[]{:S(2)}) copy-start(bf16[32,32,256]{2,1,0:T(8,128)(2,1)} %param.20) | copy-start | bytes 1572868
  0.0 14.0 %copy-start.2 = (f32[9,1024]{1,0:T(8,128)S(1)}, f32[9,1024]{1,0:T(8,128)}, u32[]{:S(2)}) copy-start(f32[9,1024]{1,0:T(8,128)} %param.25) | copy-start | bytes 110596
  1.1 13.5 %collective-permute-start = (bf16[32,1,256]{2,1,0:T(2,128)(2,1)S(1)}, bf16[32,1,256]{2,1,0:T(2,128)(2,1)S(1)}, u32[]{:S(2)}, u32[]{:S(2)}) collective-permute-start(bf16[32,1,256]{2,1,0:T(2,128)(2,1)S(1)} %get-tuple-element.7), channel_id=1, source_target_pairs={{0,2},{2,4},{4,6},{6,8},{8,10},{10,12},{12,14},{1,3},{3,5},{5,7},{... | collective-permute-start | bytes 49160 | tf_op jit(solution)/shard_map/ppermute | solution.py:22
  5.1 9.5 %collective-permute-start.1 = (bf16[32,1,256]{2,1,0:T(2,128)(2,1)S(1)}, bf16[32,1,256]{2,1,0:T(2,128)(2,1)S(1)}, u32[]{:S(2)}, u32[]{:S(2)}) collective-permute-start(bf16[32,1,256]{2,1,0:T(2,128)(2,1)S(1)} %get-tuple-element.8), channel_id=1, source_target_pairs={{2,0},{4,2},{6,4},{8,6},{10,8},{12,10},{14,12},{3,1},{5,3},{7,5},{... | collective-permute-start | bytes 49160 | tf_op jit(solution)/shard_map/ppermute | solution.py:23
  14.7 9.7 %collective-permute-start.2 = (bf16[1,34,256]{2,1,0:T(8,128)(2,1)S(1)}, bf16[1,34,256]{2,1,0:T(8,128)(2,1)}, u32[]{:S(2)}, u32[]{:S(2)}) collective-permute-start(bf16[1,34,256]{2,1,0:T(8,128)(2,1)S(1)} %get-tuple-element.5), channel_id=1, source_target_pairs={{0,1},{2,3},{4,5},{6,7},{8,9},{10,11},{12,13},{14,15},{16,17},{18,... | collective-permute-start | bytes 52232 | tf_op jit(solution)/shard_map/ppermute | solution.py:22
  16.0 8.5 %collective-permute-start.3 = (bf16[1,34,256]{2,1,0:T(8,128)(2,1)S(1)}, bf16[1,34,256]{2,1,0:T(8,128)(2,1)}, u32[]{:S(2)}, u32[]{:S(2)}) collective-permute-start(bf16[1,34,256]{2,1,0:T(8,128)(2,1)S(1)} %get-tuple-element.6), channel_id=1, source_target_pairs={{1,0},{3,2},{5,4},{7,6},{9,8},{11,10},{13,12},{15,14},{17,16},{19,... | collective-permute-start | bytes 52232 | tf_op jit(solution)/shard_map/ppermute | solution.py:23
  24.4 3.5 %copy-start.3 = (f32[1,1024]{1,0:T(1,128)S(1)}, f32[1,1024]{1,0:T(1,128)}, u32[]{:S(2)}) copy-start(f32[1,1024]{1,0:T(1,128)} %get-tuple-element.17) | copy-start | bytes 12292
  24.4 3.5 %copy-start.4 = (bf16[1024,256]{1,0:T(8,128)(2,1)S(1)}, bf16[1024,256]{1,0:T(8,128)(2,1)}, u32[]{:S(2)}) copy-start(bf16[1024,256]{1,0:T(8,128)(2,1)} %param.27) | copy-start | bytes 1572868
  24.4 3.5 %copy-start.5 = (f32[1024]{0:T(1024)S(1)}, f32[1024]{0:T(1024)}, u32[]{:S(2)}) copy-start(f32[1024]{0:T(1024)} %param.26) | copy-start | bytes 12292
  24.4 3.5 %copy-start.6 = (f32[256]{0:T(256)S(1)}, f32[256]{0:T(256)}, u32[]{:S(2)}) copy-start(f32[256]{0:T(256)} %param.28) | copy-start | bytes 3076

commit v2 on v1

v2 whole, which is shorter than its diff:
```python
import functools

import jax
import jax.numpy as jnp
from jax import lax
from jax.experimental import pallas as pl
from jax.experimental.pallas import tpu as pltpu
from jax.sharding import PartitionSpec as P

GRID = 8
EPSILON = 1e-05
MESH = pl.DeviceIdType.MESH


def gelu_tanh(inputs):
    return jax.nn.gelu(inputs, approximate=True)


def layer_norm(inputs, norm_gain, norm_shift):
    center = jnp.mean(inputs, axis=-1, keepdims=True)
    spread = jnp.mean(jnp.square(inputs - center), axis=-1, keepdims=True)
    return (inputs - center) * lax.rsqrt(spread + EPSILON) * norm_gain + norm_shift


def place_bias(rel_table):
    heads = rel_table.shape[0]
    side = 2 * GRID - 1
    table = rel_table.reshape(heads, side, side)
    shape = (side, GRID, GRID)
    entry = lax.broadcasted_iota(jnp.int32, shape, 0)
    key = lax.broadcasted_iota(jnp.int32, shape, 1)
    query = lax.broadcasted_iota(jnp.int32, shape, 2)
    onehot = (entry == GRID - 1 + query - key).astype(jnp.float32)
    by_col = jnp.einsum("hde,eki->dkhi", table, onehot, precision=lax.Precision.HIGHEST)
    by_col = by_col.reshape(side, GRID, heads * GRID)
    return jnp.concatenate([by_col[:-1], by_col[1:]], axis=-1)


def dot(a, b):
    return jnp.dot(a, b, preferred_element_type=jnp.float32)


def block_kernel(
    strips,
    col_groups,
    head_count,
    image_ref,
    bng_ref,
    bns_ref,
    wexp_ref,
    bexp_ref,
    wdep_ref,
    bdep_ref,
    wproj_ref,
    bproj_ref,
    ag_ref,
    as_ref,
    wqkv_ref,
    wout_ref,
    bias_ref,
    fg_ref,
    fs_ref,
    wup_ref,
    bup_ref,
    wdown_ref,
    bdown_ref,
    out_ref,
    edge,
    cols_in,
    rows_in,
    rim,
    e_s,
    h_s,
    sec_ref,
    arr,
    q_s,
    k_s,
    v_s,
    ctx_s,
    outb,
    sec2,
    send1,
    recv1,
    send2,
    recv2,
    hsend,
    hrecv,
):
    grid_rows, _, cols, chans = sec_ref.shape
    part = cols // strips
    rows = image_ref.shape[0]
    piece = ctx_s.shape[1]
    blocks = GRID * GRID // piece
    per_block = piece // GRID
    head_size = chans // head_count
    me_s = lax.axis_index("strip")
    tile = lax.axis_index("tile")
    me_k = tile // col_groups
    within = tile % col_groups
    peers = strips * GRID

    def device(s, k):
        return {"strip": s, "tile": k * col_groups + within}

    def is_me(s, k):
        return jnp.logical_and(s == me_s, k == me_k)

    barrier = pltpu.get_barrier_semaphore()
    for m in range(1, peers):
        s, k = (me_s + m // GRID) % strips, (me_k + m) % GRID
        pl.semaphore_signal(barrier, inc=1, device_id=device(s, k), device_id_type=MESH)
    tiles = GRID * col_groups
    sides = ((tile + tiles - 1) % tiles, (tile + 1) % tiles)
    for t in sides:
        for s in range(strips):
            pl.semaphore_signal(
                barrier, inc=1, device_id={"strip": s, "tile": t}, device_id_type=MESH
            )
    pl.semaphore_wait(barrier, peers - 1 + 2 * strips)

    edge[0] = image_ref[:, 0:16, :].astype(jnp.float32)[:, 0, :].astype(jnp.bfloat16)
    edge[1] = image_ref[:, cols - 16 : cols, :].astype(jnp.float32)[:, 15, :].astype(jnp.bfloat16)
    halo = []
    for i in range(2):
        for s in range(strips):
            halo.append(
                pltpu.make_async_remote_copy(
                    edge.at[i],
                    cols_in.at[1 - i, me_s],
                    hsend.at[i, s],
                    hrecv.at[1 - i, me_s],
                    device_id={"strip": s, "tile": sides[i]},
                    device_id_type=MESH,
                )
            )
    for i in range(2):
        halo.append(
            pltpu.make_async_remote_copy(
                image_ref.at[(rows - 1) * (1 - i)],
                rows_in.at[i],
                hsend.at[2, i],
                hrecv.at[2, i],
                device_id={"strip": (me_s + 1 + i * (strips - 2)) % strips, "tile": tile},
                device_id_type=MESH,
            )
        )
    for copy in halo:
        copy.start()

    lanes = 128
    chunks = wexp_ref.shape[1] // lanes
    pad = 8
    group = 4

    def expand(pixels):
        normed = (pixels.astype(jnp.float32) * bng_ref[...] + bns_ref[...]).astype(jnp.bfloat16)
        return gelu_tanh(dot(normed, wexp_ref[...]) + bexp_ref[...])

    @pl.loop(0, rows // group)
    def _(q):
        pixels = image_ref[pl.ds(group * q, group)].reshape(group * cols, chans)
        act = expand(pixels)
        for c in range(chunks):
            e_s[pl.ds(group * q + 1, group), c, pad : pad + cols, :] = act[
                :, lanes * c : lanes * (c + 1)
            ].reshape(group, cols, lanes)

    for i in range(2):
        for s in range(strips):
            pltpu.make_async_copy(cols_in.at[i, s], cols_in.at[i, s], hrecv.at[i, s]).wait()
        pltpu.make_async_copy(rows_in.at[i], rows_in.at[i], hrecv.at[2, i]).wait()
    row_ok = (
        jnp.where(me_s > 0, 1.0, 0.0),
        jnp.where(me_s < strips - 1, 1.0, 0.0),
    )
    col_ok = (
        jnp.where(tile > 0, 1.0, 0.0),
        jnp.where(tile < tiles - 1, 1.0, 0.0),
    )
    for i in range(2):
        act = expand(rows_in[i]) * row_ok[i]
        for c in range(chunks):
            e_s[(rows + 1) * i, c, pad : pad + cols, :] = act[:, lanes * c : lanes * (c + 1)]
        act = expand(cols_in[i].reshape(strips * rows, chans)) * col_ok[i]
        rim[i, 0:8] = jnp.zeros((8, act.shape[1]), jnp.float32)
        rim[i, 8 : 8 + strips * rows] = act
        rim[i, 8 + strips * rows :] = jnp.zeros((8, act.shape[1]), jnp.float32)

    for i in range(2):
        at = (pad + cols) * i

        @pl.loop(0, rows + 2)
        def _(r):
            line = rim[i, pl.ds(me_s * rows + 7 + r, 1), :]
            for c in range(chunks):
                e_s[r, c, at : at + 8, :] = jnp.broadcast_to(
                    line[:, lanes * c : lanes * (c + 1)], (8, lanes)
                )

    def first_copy(s, k, g):
        src = sec_ref.at[g, k, pl.ds(part * s, part)]
        dst = arr.at[grid_rows * me_s + g, me_k]
        return (
            lambda: pltpu.make_async_remote_copy(
                src,
                dst,
                send1.at[s, k],
                recv1.at[me_s, me_k],
                device_id=device(s, k),
                device_id_type=MESH,
            ),
            lambda: pltpu.make_async_copy(src, dst, recv1.at[me_s, me_k]),
        )

    groups = rows // group
    per_grid = groups // grid_rows
    far = (me_k // (GRID // per_grid) + 1) % per_grid

    @pl.loop(0, groups)
    def _(m):
        g = m % grid_rows
        sub = (far + m // grid_rows) % per_grid
        q = per_grid * g + sub
        for c in range(chunks):
            at = slice(lanes * c, lanes * (c + 1))
            acc = [jnp.broadcast_to(bdep_ref[:, at], (cols, lanes))] * group
            for r in range(group + 2):
                for j in range(3):
                    v = e_s[group * q + r, c, pad - 1 + j : pad - 1 + j + cols, :]
                    for o in range(group):
                        if 0 <= r - o <= 2:
                            tap = 3 * (r - o) + j
                            acc[o] = acc[o] + v * wdep_ref[tap : tap + 1, at]
            for o in range(group):
                h_s[cols * o : cols * (o + 1), at] = gelu_tanh(acc[o]).astype(jnp.bfloat16)
        skip = image_ref[pl.ds(group * q, group)].reshape(group * cols, chans).astype(jnp.float32)
        sec = skip + dot(h_s[...], wproj_ref[...]) + bproj_ref[...]
        sec_ref[g, pl.ds(group * sub, group)] = sec.astype(jnp.bfloat16).reshape(
            group, cols, chans
        )
        for r in range(group):
            for s in range(strips):
                k = group * sub + r
                remote, own = first_copy(s, k, g)

                @pl.when(jnp.logical_not(is_me(s, k)))
                def _():
                    remote().start()

                @pl.when(is_me(s, k))
                def _():
                    own().start()

    def wait_first(s, k):
        piece_ref = arr.at[pl.ds(grid_rows * s, grid_rows), k]
        pltpu.make_async_copy(piece_ref, piece_ref, recv1.at[s, k]).wait()

    span = piece * part
    row_id = lax.broadcasted_iota(jnp.int32, (span, span), 0)
    col_id = lax.broadcasted_iota(jnp.int32, (span, span), 1)
    swap = jnp.where(col_id == (row_id % piece) * part + row_id // piece, 1.0, 0.0).astype(
        jnp.bfloat16
    )
    lane_head = lax.broadcasted_iota(jnp.int32, (head_count * piece, chans), 1) // head_size
    row_id = lax.broadcasted_iota(jnp.int32, (head_count * piece, chans), 0)
    row_head = row_id // GRID % head_count
    mask = jnp.where(lane_head == row_head, 1.0, 0.0)
    mask_bf = mask.astype(jnp.bfloat16)

    blocks_per_strip = blocks // strips
    for b in range(blocks):
        if b % blocks_per_strip == 0:
            for k in range(GRID):
                wait_first(b // blocks_per_strip, k)
        x = arr[per_block * b : per_block * (b + 1)].reshape(span, chans).astype(jnp.float32)
        normed = layer_norm(x, ag_ref[...], as_ref[...]).astype(jnp.bfloat16)
        normed = dot(swap, normed).astype(jnp.bfloat16)
        qkv = dot(normed, wqkv_ref[...])
        q = (qkv[:, :chans] * head_size ** (-0.5)).reshape(part, per_block, GRID, chans)
        q_s[b] = jnp.concatenate([q, q], axis=2).astype(jnp.bfloat16)
        k_s[:, piece * b : piece * (b + 1), :] = (
            qkv[:, chans : 2 * chans].astype(jnp.bfloat16).reshape(part, piece, chans)
        )
        v_s[:, piece * b : piece * (b + 1), :] = (
            qkv[:, 2 * chans :].astype(jnp.bfloat16).reshape(part, piece, chans)
        )

    def back_copy(b, k):
        s = b // blocks_per_strip
        half = b % blocks_per_strip
        src = outb.at[pl.ds(per_block * b, per_block), k]
        dst = sec2.at[pl.ds(per_block * half, per_block), me_k, pl.ds(part * me_s, part)]
        return (
            s,
            lambda: pltpu.make_async_remote_copy(
                src,
                dst,
                send2.at[b, k],
                recv2.at[half, me_s, me_k],
                device_id=device(s, k),
                device_id_type=MESH,
            ),
            lambda: pltpu.make_async_copy(src, dst, recv2.at[half, me_s, me_k]),
        )

    for b in range(blocks):
        bias = jnp.concatenate(
            [bias_ref[GRID - 1 + per_block * b - k] for k in range(GRID)], axis=0
        )
        for w in range(part):
            qbd = (
                jnp.concatenate(
                    [q_s[b, w, i] for i in range(per_block) for _ in range(head_count // 2)], axis=0
                )
                * mask_bf
            )
            s = lax.dot_general(
                k_s[w], qbd, (((1,), (1,)), ((), ())), preferred_element_type=jnp.float32
            )
            s = s + bias
            e = jnp.exp(s - jnp.max(s, axis=0, keepdims=True))
            p = (e * (1.0 / jnp.sum(e, axis=0, keepdims=True))).astype(jnp.bfloat16)
            o = lax.dot_general(
                p, v_s[w], (((0,), (0,)), ((), ())), preferred_element_type=jnp.float32
            )
            o = (o * mask).reshape(per_block, head_count, GRID, chans)
            ctx_s[w] = jnp.sum(o, axis=1).reshape(piece, chans).astype(jnp.bfloat16)
        ctx = dot(swap, ctx_s[...].reshape(span, chans)).astype(jnp.bfloat16)
        x = arr[per_block * b : per_block * (b + 1)].reshape(span, chans).astype(jnp.float32)
        attended = (x + dot(ctx, wout_ref[...])).astype(jnp.bfloat16)
        outb[per_block * b : per_block * (b + 1)] = attended.reshape(per_block, GRID, part, chans)
        for m in range(GRID):
            k = (me_k + m) % GRID
            s, remote, own = back_copy(b, k)

            @pl.when(jnp.logical_not(is_me(s, k)))
            def _():
                remote().start()

            @pl.when(is_me(s, k))
            def _():
                own().start()

    pairs = GRID // 2
    for m in range(pairs):
        pair = (me_k // 2 + m) % pairs
        for s in range(strips):
            for kk in range(2):
                k = 2 * pair + kk
                for half in range(blocks_per_strip):
                    ref = sec2.at[pl.ds(per_block * half, per_block), k, pl.ds(part * s, part)]
                    pltpu.make_async_copy(ref, ref, recv2.at[half, s, k]).wait()
        x = sec2[:, pl.ds(2 * pair, 2)].reshape(grid_rows * 2 * cols, chans).astype(jnp.float32)
        normed = layer_norm(x, fg_ref[...], fs_ref[...]).astype(jnp.bfloat16)
        hidden = gelu_tanh(dot(normed, wup_ref[...]) + bup_ref[...]).astype(jnp.bfloat16)
        res = x + dot(hidden, wdown_ref[...]) + bdown_ref[...]
        out_ref[:, pl.ds(2 * pair, 2)] = res.reshape(grid_rows, 2, cols, chans)

    for copy in halo:
        copy.wait_send()
    for s in range(strips):
        for k in range(GRID):

            @pl.when(jnp.logical_not(is_me(s, k)))
            def _():
                src = sec_ref.at[:, k, pl.ds(part * s, part)]
                dst = arr.at[pl.ds(grid_rows * me_s, grid_rows), me_k]
                pltpu.make_async_remote_copy(
                    src,
                    dst,
                    send1.at[s, k],
                    recv1.at[me_s, me_k],
                    device_id=device(s, k),
                    device_id_type=MESH,
                ).wait_send()

    for b in range(blocks):
        for k in range(GRID):
            s, remote, own = back_copy(b, k)

            @pl.when(jnp.logical_not(is_me(s, k)))
            def _():
                remote().wait_send()


def local(
    image,
    bn_gain,
    bn_shift,
    w_expand,
    b_expand,
    w_depth,
    b_depth,
    w_project,
    b_project,
    attn_gain,
    attn_shift,
    w_qkv,
    w_out,
    rel_table,
    ffn_gain,
    ffn_shift,
    w_up,
    b_up,
    w_down,
    b_down,
):
    tile_rows, tile_cols, channels = image.shape
    strips = lax.axis_size("strip")
    tile_count = lax.axis_size("tile")
    grid_rows = GRID // strips
    across = tile_rows // grid_rows
    col_groups = tile_count // GRID
    heads = rel_table.shape[0]
    part = tile_cols // strips
    piece = part
    blocks = GRID * GRID // piece
    bias = place_bias(rel_table)
    hidden = w_expand.shape[1]
    bf, f32 = jnp.bfloat16, jnp.float32
    vmem = pl.BlockSpec(memory_space=pltpu.VMEM)
    out = pl.pallas_call(
        functools.partial(block_kernel, strips, col_groups, heads),
        out_shape=jax.ShapeDtypeStruct((grid_rows, across, tile_cols, channels), f32),
        in_specs=[vmem] * 20,
        out_specs=vmem,
        scratch_shapes=[
            pltpu.VMEM((2, tile_rows, channels), bf),
            pltpu.VMEM((2, strips, tile_rows, channels), bf),
            pltpu.VMEM((2, tile_cols, channels), bf),
            pltpu.VMEM((2, strips * tile_rows + 16, hidden), f32),
            pltpu.VMEM((tile_rows + 2, hidden // 128, tile_cols + 16, 128), f32),
            pltpu.VMEM((4 * tile_cols, hidden), bf),
            pltpu.VMEM((grid_rows, across, tile_cols, channels), bf),
            pltpu.VMEM((GRID, GRID, part, channels), bf),
            pltpu.VMEM((blocks, part, piece // GRID, 2 * GRID, channels), bf),
            pltpu.VMEM((part, GRID * GRID, channels), bf),
            pltpu.VMEM((part, GRID * GRID, channels), bf),
            pltpu.VMEM((part, piece, channels), bf),
            pltpu.VMEM((GRID, GRID, part, channels), bf),
            pltpu.VMEM((grid_rows, GRID, tile_cols, channels), bf),
            pltpu.SemaphoreType.DMA((strips, GRID)),
            pltpu.SemaphoreType.DMA((strips, GRID)),
            pltpu.SemaphoreType.DMA((blocks, GRID)),
            pltpu.SemaphoreType.DMA((blocks // strips, strips, GRID)),
            pltpu.SemaphoreType.DMA((3, 2)),
            pltpu.SemaphoreType.DMA((3, 2)),
        ],
        compiler_params=pltpu.CompilerParams(collective_id=0, has_side_effects=True),
    )(
        image,
        bn_gain.reshape(1, -1),
        bn_shift.reshape(1, -1),
        w_expand,
        b_expand.reshape(1, -1),
        w_depth,
        b_depth.reshape(1, -1),
        w_project,
        b_project.reshape(1, -1),
        attn_gain.reshape(1, -1),
        attn_shift.reshape(1, -1),
        w_qkv,
        w_out,
        bias,
        ffn_gain.reshape(1, -1),
        ffn_shift.reshape(1, -1),
        w_up,
        b_up.reshape(1, -1),
        w_down,
        b_down.reshape(1, -1),
    )
    return out.astype(bf).reshape(tile_rows, tile_cols, channels)


def solution(mesh):
    return jax.shard_map(
        local,
        mesh=mesh,
        in_specs=(P(("group", "strip"), "tile", None),) + (P(),) * 19,
        out_specs=P(("group", "strip"), "tile", None),
        check_vma=False,
    )
```

time: 74.4 us -> 49.6 us (0.67)
  local copies, waits for them, and re-layouts: 15.3 us -> 1.18 us
  starting transfers between devices: 10.7 us -> 0 us
  matrix products: 10.7 us -> 0.43 us
  Pallas kernels: 37 us -> 44.9 us
  other arithmetic: 0.1 us -> 2.82 us
    ppermute x4 -> x0, starting transfers between devices: 10.7 us -> none  [the longest x2 5.52 us: padded(): after = lax.ppermute(initial, axis, down)]
    dot_general x2 -> x1, matrix products: 10.7 us -> 0.43 us  [place_bias(): jnp.einsum('hde,eki->dkhi', table, onehot, precision=lax.Precision.HIGHEST)]
    pallas_call x1, Pallas kernels: 37 us -> 44.9 us  [local(): pl.pallas_call(functools.partial(block_kernel, strips, col_groups, heads)...]
    unnamed x29 -> x2, local copies, waits for them, and re-layouts: 7.89 us -> 0.69 us
    another operation x3 -> x0, local copies, waits for them, and re-layouts: 3.51 us -> none  [the longest x2 3.51 us: place_bias(): jnp.stack([by_row[..., GRID - 1 - k:2 * GRID - 1 - k] for k in range(GRID...]
    convert_element_type x0 -> x1, other arithmetic: none -> 2.1 us  [local(): return out.astype(bf).reshape(tile_rows, tile_cols, channels)]
    slice x2 -> x3, local copies, waits for them, and re-layouts: 1.74 us -> 0.41 us  [place_bias(): return jnp.concatenate([by_col[:-1], by_col[1:]], axis=-1)]
    reshape x2 -> x0, local copies, waits for them, and re-layouts: 1.32 us -> none  [the longest x1 0.77 us: place_bias(): by_col.transpose(2, 0, 1, 3)]
  transfers between devices with their start and end apart: 4 -> 0, of which waited for: 0 -> 0; matrix products, arithmetic and copies ran while one was open for 17% -> 0% of each run, Pallas kernels for 0% -> 0%
where the time goes in v2:
time: 49.6 us; the launch traced here: 49.4 us
  Pallas kernels  44.9 us (91%)
  other arithmetic  2.82 us (6%)
  local copies, waits for them, and re-layouts  1.18 us (2%)
    pallas_call x1, Pallas kernels, local(): pl.pallas_call(functools.partial(block_kernel, strips, col_groups, heads)...  44.9 us
    convert_element_type x1, other arithmetic, local(): return out.astype(bf).reshape(tile_rows, tile_cols, channels)  2.1 us

profile of v2, /device:TPU:1, one launch (start us, length us, event | category | flops | bytes accessed | tf_op | source)
XLA Modules:
  0.0 49.4 jit_solution(9518084926340572344)
XLA Ops:
  0.0 0.0 copy-start
  0.0 0.7 %copy-done = f32[8,225]{1,0:T(8,128)S(1)} copy-done((f32[8,225]{1,0:T(8,128)S(1)}, f32[8,225]{1,0:T(8,128)}, u32[]{:S(2)}) %copy-start) | copy-done | bytes 7224
  0.7 0.1 reshape.56
  0.8 0.4 convolution_bitcast_fusion
  1.2 0.1 slice_bitcast_fusion.1
  1.4 0.1 copy.23
  1.5 0.1 copy.24
  1.6 0.7 %pad_maximum_fusion.bias_ref = f32[14,8,128]{2,1,0:T(8,128)} fusion(f32[14,8,64]{2,1,0:T(8,128)S(1)} %copy.24, f32[14,8,64]{2,1,0:T(8,128)S(1)} %copy.23), kind=kLoop, calls=%fused_computation.3 | loop fusion | flops 14336 | bytes 114688 | tf_op jit(solution)/shard_map/concatenate | solution.py:36
  2.4 44.9 %shard_map.190 = f32[4,8,32,256]{3,2,1,0:T(8,128)} custom-call(bf16[32,32,256]{2,1,0:T(8,128)(2,1)} %image_ref.1, f32[1,256]{1,0:T(1,128)} %bitcast.27, f32[1,256]{1,0:T(1,128)} %bitcast.28, bf16[256,1024]{1,0:T(8,128)(2,1)} %wexp_ref.1, f32[1,1024]{1,0:T(1,128)} %bitcast.24, f32[9,1024]{1,0:T(8,128)} %wdep_ref.1, f32[1,1024]{1,0:T(1,128)} %bitcast.25, ...), custom_call_target="tpu_custom_call" | custom-call | tf_op jit(solution)/shard_map/pallas_call | solution.py:422
  47.3 2.1 %convert_element_type.4 = bf16[4,8,32,256]{3,2,1,0:T(8,128)(2,1)} convert(f32[4,8,32,256]{3,2,1,0:T(8,128)} %shard_map.190) | non-fusion elementwise | flops 262144 | bytes 1572864 | tf_op jit(solution)/shard_map/convert_element_type | solution.py:472
  (1 shorter events, 0.0 us)
Async XLA Ops:
  0.0 0.7 %copy-start = (f32[8,225]{1,0:T(8,128)S(1)}, f32[8,225]{1,0:T(8,128)}, u32[]{:S(2)}) copy-start(f32[8,225]{1,0:T(8,128)} %param.33) | copy-start | bytes 21604

commit v3 on v2

--- a/solution.py
+++ b/solution.py
@@ -10,6 +10,7 @@
 GRID = 8
 EPSILON = 1e-05
 MESH = pl.DeviceIdType.MESH
+ORDER = (4, 5, 3, 2, 6, 1, 7, 0)
 
 
 def gelu_tanh(inputs):
@@ -156,14 +157,20 @@
         normed = (pixels.astype(jnp.float32) * bng_ref[...] + bns_ref[...]).astype(jnp.bfloat16)
         return gelu_tanh(dot(normed, wexp_ref[...]) + bexp_ref[...])
 
-    @pl.loop(0, rows // group)
-    def _(q):
+    groups = rows // group
+    ahead = 3
+
+    def expand_rows(q):
         pixels = image_ref[pl.ds(group * q, group)].reshape(group * cols, chans)
         act = expand(pixels)
         for c in range(chunks):
             e_s[pl.ds(group * q + 1, group), c, pad : pad + cols, :] = act[
                 :, lanes * c : lanes * (c + 1)
             ].reshape(group, cols, lanes)
+
+    @pl.loop(0, ahead)
+    def _(q):
+        expand_rows(q)
 
     for i in range(2):
         for s in range(strips):
@@ -212,15 +219,16 @@
             lambda: pltpu.make_async_copy(src, dst, recv1.at[me_s, me_k]),
         )
 
-    groups = rows // group
     per_grid = groups // grid_rows
-    far = (me_k // (GRID // per_grid) + 1) % per_grid
 
     @pl.loop(0, groups)
-    def _(m):
-        g = m % grid_rows
-        sub = (far + m // grid_rows) % per_grid
-        q = per_grid * g + sub
+    def _(q):
+        @pl.when(q + ahead < groups)
+        def _():
+            expand_rows(q + ahead)
+
+        g = q // per_grid
+        sub = q % per_grid
         for c in range(chunks):
             at = slice(lanes * c, lanes * (c + 1))
             acc = [jnp.broadcast_to(bdep_ref[:, at], (cols, lanes))] * group
@@ -285,9 +293,13 @@
             qkv[:, 2 * chans :].astype(jnp.bfloat16).reshape(part, piece, chans)
         )
 
-    def back_copy(b, k):
-        s = b // blocks_per_strip
-        half = b % blocks_per_strip
+    def block_of(i):
+        s = (me_s + 1 + i % strips) % strips
+        half = i // strips
+        return s, half, blocks_per_strip * s + half
+
+    def back_copy(i, k):
+        s, half, b = block_of(i)
         src = outb.at[pl.ds(per_block * b, per_block), k]
         dst = sec2.at[pl.ds(per_block * half, per_block), me_k, pl.ds(part * me_s, part)]
         return (
@@ -295,7 +307,7 @@
             lambda: pltpu.make_async_remote_copy(
                 src,
                 dst,
-                send2.at[b, k],
+                send2.at[i, k],
                 recv2.at[half, me_s, me_k],
                 device_id=device(s, k),
                 device_id_type=MESH,
@@ -303,14 +315,15 @@
             lambda: pltpu.make_async_copy(src, dst, recv2.at[half, me_s, me_k]),
         )
 
-    for b in range(blocks):
+    for i in range(blocks):
+        b = block_of(i)[2]
         bias = jnp.concatenate(
             [bias_ref[GRID - 1 + per_block * b - k] for k in range(GRID)], axis=0
         )
         for w in range(part):
             qbd = (
                 jnp.concatenate(
-                    [q_s[b, w, i] for i in range(per_block) for _ in range(head_count // 2)], axis=0
+                    [q_s[b, w, j] for j in range(per_block) for _ in range(head_count // 2)], axis=0
                 )
                 * mask_bf
             )
@@ -326,12 +339,12 @@
             o = (o * mask).reshape(per_block, head_count, GRID, chans)
             ctx_s[w] = jnp.sum(o, axis=1).reshape(piece, chans).astype(jnp.bfloat16)
         ctx = dot(swap, ctx_s[...].reshape(span, chans)).astype(jnp.bfloat16)
-        x = arr[per_block * b : per_block * (b + 1)].reshape(span, chans).astype(jnp.float32)
+        x = arr[pl.ds(per_block * b, per_block)].reshape(span, chans).astype(jnp.float32)
         attended = (x + dot(ctx, wout_ref[...])).astype(jnp.bfloat16)
-        outb[per_block * b : per_block * (b + 1)] = attended.reshape(per_block, GRID, part, chans)
-        for m in range(GRID):
+        outb[pl.ds(per_block * b, per_block)] = attended.reshape(per_block, GRID, part, chans)
+        for m in ORDER:
             k = (me_k + m) % GRID
-            s, remote, own = back_copy(b, k)
+            s, remote, own = back_copy(i, k)
 
             @pl.when(jnp.logical_not(is_me(s, k)))
             def _():
@@ -374,9 +387,9 @@
                     device_id_type=MESH,
                 ).wait_send()
 
-    for b in range(blocks):
+    for i in range(blocks):
         for k in range(GRID):
-            s, remote, own = back_copy(b, k)
+            s, remote, own = back_copy(i, k)
 
             @pl.when(jnp.logical_not(is_me(s, k)))
             def _():
@@ -446,7 +459,9 @@
             pltpu.SemaphoreType.DMA((3, 2)),
             pltpu.SemaphoreType.DMA((3, 2)),
         ],
-        compiler_params=pltpu.CompilerParams(collective_id=0, has_side_effects=True),
+        compiler_params=pltpu.CompilerParams(
+            collective_id=0, has_side_effects=True, vmem_limit_bytes=24 * 2**20
+        ),
     )(
         image,
         bn_gain.reshape(1, -1),

time: 49.6 us -> 51.6 us (1.040); the launches traced: 49.4 us -> 50.8 us
  local copies, waits for them, and re-layouts: 1.18 us -> 4.89 us
  other arithmetic: 2.82 us -> 0.95 us
  Pallas kernels: 44.9 us -> 44.3 us
    unnamed x2 -> x40, local copies, waits for them, and re-layouts: 0.69 us -> 4.41 us
    convert_element_type x1, other arithmetic: 2.1 us -> 0.87 us  [local(): return out.astype(bf).reshape(tile_rows, tile_cols, channels)]
    concatenate x1, other arithmetic: 0.72 us -> 0.08 us  [place_bias(): return jnp.concatenate([by_col[:-1], by_col[1:]], axis=-1)]
    pallas_call x1, Pallas kernels: 44.9 us -> 44.3 us  [local(): pl.pallas_call(functools.partial(block_kernel, strips, col_groups, heads)...]
where the time goes in v3:
time: 51.6 us; the launch traced here: 50.8 us
  Pallas kernels  44.3 us (86%)
  local copies, waits for them, and re-layouts  4.89 us (9%)
  other arithmetic  0.95 us (2%)
    pallas_call x1, Pallas kernels, local(): pl.pallas_call(functools.partial(block_kernel, strips, col_groups, heads)...  44.3 us
    unnamed x40, local copies, waits for them, and re-layouts  4.41 us

profile of v3, /device:TPU:1, one launch (start us, length us, event | category | flops | bytes accessed | tf_op | source)
XLA Modules:
  0.0 50.8 jit_solution(855281153312407874)
XLA Ops:
  0.0 0.7 %copy-done.19 = f32[8,225]{1,0:T(8,128)S(1)} copy-done((f32[8,225]{1,0:T(8,128)S(1)}, f32[8,225]{1,0:T(8,128)}, u32[]{:S(2)}) %copy-start.19) | copy-done | bytes 7224
  0.7 0.1 reshape.56
  0.8 0.0 copy-start.3
  0.8 0.4 convolution_bitcast_fusion
  1.2 0.0 copy-start.1
  1.3 0.0 copy-start.2
  1.3 0.1 slice_bitcast_fusion.1
  1.4 0.0 copy-start
  1.4 0.1 copy.23
  1.5 0.1 copy.24
  1.7 0.0 copy-start.8
  1.7 0.0 copy-start.9
  1.7 0.0 copy-start.10
  1.7 0.0 copy-start.11
  1.7 0.0 copy-start.12
  1.8 0.0 copy-start.13
  1.8 0.0 copy-start.14
  1.8 0.0 copy-start.15
  1.8 0.0 copy-start.16
  1.8 0.0 copy-start.17
  1.8 0.0 copy-start.18
  1.8 0.1 pad_maximum_fusion.bias_ref
  1.9 0.4 copy-done.1
  2.3 0.2 copy-done.2
  2.5 0.2 copy-done
  2.7 0.0 copy-done.11
  2.8 0.0 copy-start.4
  2.8 1.0 %copy-done.4 = bf16[1024,256]{1,0:T(8,128)(2,1)S(1)} copy-done((bf16[1024,256]{1,0:T(8,128)(2,1)S(1)}, bf16[1024,256]{1,0:T(8,128)(2,1)}, u32[]{:S(2)}) %copy-start.4) | copy-done | bytes 524312
  3.8 1.0 %copy-done.5 = bf16[256,768]{1,0:T(8,128)(2,1)S(1)} copy-done((bf16[256,768]{1,0:T(8,128)(2,1)S(1)}, bf16[256,768]{1,0:T(8,128)(2,1)}, u32[]{:S(2)}) %copy-start.5) | copy-done | bytes 393240
  4.8 0.8 %copy-done.7 = f32[9,1024]{1,0:T(8,128)S(1)} copy-done((f32[9,1024]{1,0:T(8,128)S(1)}, f32[9,1024]{1,0:T(8,128)}, u32[]{:S(2)}) %copy-start.7) | copy-done | bytes 36888
  5.7 44.3 %shard_map.190 = f32[4,8,32,256]{3,2,1,0:T(8,128)S(1)} custom-call(bf16[32,32,256]{2,1,0:T(8,128)(2,1)S(1)} %copy-done, f32[1,256]{1,0:T(1,128)S(1)} %bitcast.27, f32[1,256]{1,0:T(1,128)S(1)} %bitcast.28, bf16[256,1024]{1,0:T(8,128)(2,1)S(1)} %copy-done.1, f32[1,1024]{1,0:T(1,128)S(1)} %bitcast.24, f32[9,1024]{1,0:T(8,128)S(1)} %copy-done.7, ...), custom_call_target="tpu_custom_call" | custom-call | tf_op jit(solution)/shard_map/pallas_call | solution.py:435
  50.0 0.9 %convert_element_type.4 = bf16[4,8,32,256]{3,2,1,0:T(8,128)(2,1)} convert(f32[4,8,32,256]{3,2,1,0:T(8,128)S(1)} %shard_map.190) | non-fusion elementwise | flops 262144 | bytes 1572864 | tf_op jit(solution)/shard_map/convert_element_type | solution.py:487
  (17 shorter events, 0.0 us)
Async XLA Ops:
  0.0 0.7 %copy-start.19 = (f32[8,225]{1,0:T(8,128)S(1)}, f32[8,225]{1,0:T(8,128)}, u32[]{:S(2)}) copy-start(f32[8,225]{1,0:T(8,128)} %param.33) | copy-start | bytes 21604
  0.7 1.2 %copy-start.6 = (bf16[256,256]{1,0:T(8,128)(2,1)S(1)}, bf16[256,256]{1,0:T(8,128)(2,1)}, u32[]{:S(2)}) copy-start(bf16[256,256]{1,0:T(8,128)(2,1)} %wout_ref.1) | copy-start | bytes 393220
  0.8 1.1 %copy-start.3 = (bf16[256,1024]{1,0:T(8,128)(2,1)S(1)}, bf16[256,1024]{1,0:T(8,128)(2,1)}, u32[]{:S(2)}) copy-start(bf16[256,1024]{1,0:T(8,128)(2,1)} %wup_ref.1) | copy-start | bytes 1572868
  1.2 1.1 %copy-start.1 = (bf16[256,1024]{1,0:T(8,128)(2,1)S(1)}, bf16[256,1024]{1,0:T(8,128)(2,1)}, u32[]{:S(2)}) copy-start(bf16[256,1024]{1,0:T(8,128)(2,1)} %wexp_ref.1) | copy-start | bytes 1572868
  1.3 1.2 %copy-start.2 = (bf16[1024,256]{1,0:T(8,128)(2,1)S(1)}, bf16[1024,256]{1,0:T(8,128)(2,1)}, u32[]{:S(2)}) copy-start(bf16[1024,256]{1,0:T(8,128)(2,1)} %wproj_ref.1) | copy-start | bytes 1572868
  1.4 1.3 %copy-start = (bf16[32,32,256]{2,1,0:T(8,128)(2,1)S(1)}, bf16[32,32,256]{2,1,0:T(8,128)(2,1)}, u32[]{:S(2)}) copy-start(bf16[32,32,256]{2,1,0:T(8,128)(2,1)} %image_ref.1) | copy-start | bytes 1572868
  1.7 1.0 %copy-start.8 = (f32[1024]{0:T(1024)S(1)}, f32[1024]{0:T(1024)}, u32[]{:S(2)}) copy-start(f32[1024]{0:T(1024)} %param.24) | copy-start | bytes 12292
  1.7 1.0 %copy-start.9 = (f32[1024]{0:T(1024)S(1)}, f32[1024]{0:T(1024)}, u32[]{:S(2)}) copy-start(f32[1024]{0:T(1024)} %param.26) | copy-start | bytes 12292
  1.7 1.0 %copy-start.10 = (f32[1024]{0:T(1024)S(1)}, f32[1024]{0:T(1024)}, u32[]{:S(2)}) copy-start(f32[1024]{0:T(1024)} %param.37) | copy-start | bytes 12292
  1.7 1.0 %copy-start.11 = (f32[256]{0:T(256)S(1)}, f32[256]{0:T(256)}, u32[]{:S(2)}) copy-start(f32[256]{0:T(256)} %param.21) | copy-start | bytes 3076
  1.7 1.0 %copy-start.12 = (f32[256]{0:T(256)S(1)}, f32[256]{0:T(256)}, u32[]{:S(2)}) copy-start(f32[256]{0:T(256)} %param.22) | copy-start | bytes 3076
  1.8 1.0 %copy-start.13 = (f32[256]{0:T(256)S(1)}, f32[256]{0:T(256)}, u32[]{:S(2)}) copy-start(f32[256]{0:T(256)} %param.28) | copy-start | bytes 3076
  1.8 1.0 %copy-start.14 = (f32[256]{0:T(256)S(1)}, f32[256]{0:T(256)}, u32[]{:S(2)}) copy-start(f32[256]{0:T(256)} %param.29) | copy-start | bytes 3076
  1.8 1.0 %copy-start.15 = (f32[256]{0:T(256)S(1)}, f32[256]{0:T(256)}, u32[]{:S(2)}) copy-start(f32[256]{0:T(256)} %param.30) | copy-start | bytes 3076
  1.8 1.0 %copy-start.16 = (f32[256]{0:T(256)S(1)}, f32[256]{0:T(256)}, u32[]{:S(2)}) copy-start(f32[256]{0:T(256)} %param.34) | copy-start | bytes 3076
  1.8 1.0 %copy-start.17 = (f32[256]{0:T(256)S(1)}, f32[256]{0:T(256)}, u32[]{:S(2)}) copy-start(f32[256]{0:T(256)} %param.35) | copy-start | bytes 3076
  1.8 1.0 %copy-start.18 = (f32[256]{0:T(256)S(1)}, f32[256]{0:T(256)}, u32[]{:S(2)}) copy-start(f32[256]{0:T(256)} %param.39) | copy-start | bytes 3076
  2.8 1.0 %copy-start.4 = (bf16[1024,256]{1,0:T(8,128)(2,1)S(1)}, bf16[1024,256]{1,0:T(8,128)(2,1)}, u32[]{:S(2)}) copy-start(bf16[1024,256]{1,0:T(8,128)(2,1)} %wdown_ref.1) | copy-start | bytes 1572868
  3.8 1.0 %copy-start.5 = (bf16[256,768]{1,0:T(8,128)(2,1)S(1)}, bf16[256,768]{1,0:T(8,128)(2,1)}, u32[]{:S(2)}) copy-start(bf16[256,768]{1,0:T(8,128)(2,1)} %wqkv_ref.1) | copy-start | bytes 1179652
  4.8 0.8 %copy-start.7 = (f32[9,1024]{1,0:T(8,128)S(1)}, f32[9,1024]{1,0:T(8,128)}, u32[]{:S(2)}) copy-start(f32[9,1024]{1,0:T(8,128)} %wdep_ref.1) | copy-start | bytes 110596
